TPU v7x, 128 devices: a whole 4x4x4 slice. The times are simulated.
128 devices in a mesh: gx: 8 (over z, core), gy: 16 (over x, y).
Axes of the slice: x: 4, y: 4, z: 4, core: 2. Of those that a mesh axis runs over, the one named last changes fastest.
Arguments:
- velocity: float32 [3, 64, 128, 128], P(None, 'gx', 'gy'), may hold values from -1 to 1
- wall_cells: int32 [64, 128, 128], P('gx', 'gy'), may hold values 0 or 1
- tile_counts: int32 [8, 16, 8], P('gx', 'gy'), may hold values from 32 to 256, as said below
- helper_tile: int32 [8, 16], P('gx'), may hold values from 0 to 127, as said below
- base_fields: float32 [8, 16, 8, 3, 32, 1024], P('gx', 'gy'), may hold values from -2.5 to 2.5
- extra_fields: float32 [8, 16, 3, 224, 1024], P('gx', 'gy'), may hold values from -6.1 to 6.1
- base_noise: bfloat16 [8, 16, 8, 2, 3, 32, 1024], P('gx', 'gy'), may hold values from -2.5 to 2.5
- extra_noise: bfloat16 [8, 16, 2, 3, 224, 1024], P('gx', 'gy'), may hold values from -2.5 to 2.5
Outputs:
- new_base_fields: float32 [8, 16, 8, 3, 32, 1024], P('gx', 'gy')
- new_extra_fields: float32 [8, 16, 3, 224, 1024], P('gx', 'gy')
- polymer_stress: float32 [8, 16, 8, 6, 1024], P('gx', 'gy')
Inputs may be any that keep to these rules, and one draw needn't show every extreme that they name: `tile_counts`: each entry is 32 or 256. In each row of tiles exactly 16 tiles have 256, these are the tiles that helper_tile names, one column of tiles holds at most 4 of them and in every row some column holds exactly 4. `helper_tile`: entry [i, h] = o * 8 + t names tile t of column o in row i; the entries of a row are distinct and name exactly the row's tiles with 256 fields.
All inputs are finite; a program needn't handle non-finite values. No bound on the sum of `wall_cells` on one device may be relied on, other than what follows from the above.
Results may differ from a plain program's by a relative error of at most 0.0003.
Values sent between devices are 32-bit elements; how exact they have to be, the bound alone decides.
A program may use at most 128 MiB of HBM per device.

v0:
```python
import math

import jax
import jax.numpy as jnp
from jax import lax
from jax.sharding import PartitionSpec as P

ALL_FIELDS = 256
STEPS = 2
HEAVY_MOST = 4


time_step = 0.05
weissenberg = 0.25
max_extension = 50.0
noise_scale = (time_step / weissenberg) ** 0.5
component_pairs = ((0, 0), (1, 1), (2, 2), (0, 1), (0, 2), (1, 2))


def extended(shard, sides, width):
    for axis, dim in sides:
        size, length = (lax.axis_size(axis), shard.shape[dim])
        up = [(i, (i + 1) % size) for i in range(size - 1)]
        down = [(j, i) for i, j in up]
        last = lax.slice_in_dim(shard, length - width, length, axis=dim)
        leading = lax.slice_in_dim(shard, 0, width, axis=dim)
        before = lax.ppermute(last, axis, up)
        after = lax.ppermute(leading, axis, down)
        shard = jnp.concatenate([before, shard, after], axis=dim)
    return shard


def in_one_piece(arrays, axis, dim, along):
    widths = [math.prod(a.shape[along:]) for a in arrays]
    both = jnp.concatenate(
        [a.reshape(*a.shape[:along], w) for a, w in zip(arrays, widths)], axis=along
    )
    out = lax.all_gather(both, axis, axis=dim, tiled=True)
    parts = jnp.split(out, [sum(widths[:k]) for k in range(1, len(widths))], axis=along)
    return tuple((b.reshape(*out.shape[:along], *a.shape[along:]) for a, b in zip(arrays, parts)))


def velocity_gradient(padded, wall_cells):
    along_x = (padded[:, 2:, 1:-1, 1:-1] - padded[:, :-2, 1:-1, 1:-1]) * 0.5
    along_y = (padded[:, 1:-1, 2:, 1:-1] - padded[:, 1:-1, :-2, 1:-1]) * 0.5
    along_z = (padded[:, 1:-1, 1:-1, 2:] - padded[:, 1:-1, 1:-1, :-2]) * 0.5
    fluid = (wall_cells == 0).astype(jnp.float32)
    stacked = jnp.stack([along_x, along_y, along_z], axis=1) * fluid
    return stacked.reshape((9,) + wall_cells.shape)


def spring_factor(total, count):
    return 1.0 / (1.0 - total / count / max_extension)


def advance(state, grad, factor, noise):
    relax = factor[..., None, :] * (0.5 / weissenberg)
    parts = []
    for component in range(3):
        drift = grad[..., 3 * component, None, :] * state[..., 0, :, :]
        drift = drift + grad[..., 3 * component + 1, None, :] * state[..., 1, :, :]
        drift = drift + grad[..., 3 * component + 2, None, :] * state[..., 2, :, :]
        current = state[..., component, :, :]
        parts.append(
            current
            + time_step * (drift - relax * current)
            + noise_scale * noise[..., component, :, :].astype(jnp.float32)
        )
    return jnp.stack(parts, axis=-3)


def moments(state):
    return jnp.stack(
        [
            jnp.sum(state[..., first_axis, :, :] * state[..., second_axis, :, :], axis=-2)
            for first_axis, second_axis in component_pairs
        ],
        axis=-2,
    )


def polymer_stress(total, count):
    second = total / count
    trace = second[..., 0, :] + second[..., 1, :] + second[..., 2, :]
    stretch = 1.0 / (1.0 - trace / max_extension)
    unit = jnp.array([1.0, 1.0, 1.0, 0.0, 0.0, 0.0], jnp.float32)[:, None]
    return (stretch[..., None, :] * second - unit) / weissenberg


def per_device(
    velocity,
    wall_cells,
    tile_counts,
    helper_tile,
    base_fields,
    extra_fields,
    base_noise,
    extra_noise,
):
    padded = extended(velocity, (("gx", 1), ("gy", 2)), 1)
    padded = jnp.pad(padded, ((0, 0), (0, 0), (0, 0), (1, 1)))
    grad_grid = velocity_gradient(padded, wall_cells)
    block_x, block_y, block_z = wall_cells.shape
    tile_count = tile_counts.shape[2]
    cell_count = base_fields.shape[-1]
    tile_grad = grad_grid.reshape(9, block_x, block_y, tile_count, block_z // tile_count)
    tile_grad = tile_grad.transpose(3, 0, 1, 2, 4).reshape(tile_count, 9, cell_count)
    group_size = lax.axis_size("gy")
    my_index = lax.axis_index("gy")
    helper_row = helper_tile[0]
    slot_range = jnp.arange(group_size, dtype=jnp.int32)
    owned_ids = my_index * tile_count + jnp.arange(tile_count, dtype=jnp.int32)
    counts = tile_counts[0, 0].astype(jnp.float32)
    heavy_tile = tile_counts[0, 0] == ALL_FIELDS
    assign = (helper_row[:, None] == owned_ids[None, :]).astype(jnp.float32)
    my_tile = jnp.sum(jnp.where(slot_range == my_index, helper_row, 0)).astype(jnp.float32)
    slot_rank = jnp.cumsum(heavy_tile.astype(jnp.int32)) - 1
    pack_map = (
        (slot_rank[None, :] == jnp.arange(HEAVY_MOST, dtype=jnp.int32)[:, None])
        & heavy_tile[None, :]
    ).astype(jnp.float32)
    packed_ids = jnp.sum(pack_map * (owned_ids.astype(jnp.float32) + 1.0)[None, :], axis=1) - 1.0
    outgoing = jnp.sum(assign[:, :, None, None] * tile_grad[None], axis=1)
    arrived = lax.all_to_all(outgoing, "gy", split_axis=0, concat_axis=0, tiled=True)
    helper_grad = jnp.sum(arrived, axis=0)

    def partner_totals(own_rows, extra_rows):
        packed_own = jnp.sum(pack_map[:, :, None, None] * own_rows[None], axis=1)
        got_own, got_ids, got_extra = (
            *in_one_piece((packed_own, packed_ids), "gy", 0, 1),
            lax.all_gather(extra_rows[None], "gy", axis=0, tiled=True),
        )
        matches = (got_ids == my_tile).astype(jnp.float32)
        helper_total = extra_rows + jnp.sum(matches[:, None, None] * got_own, axis=0)
        tile_total = own_rows + jnp.sum(assign.T[:, :, None, None] * got_extra[None], axis=1)
        return (tile_total, helper_total)

    base_state = base_fields[0, 0]
    extra_state = extra_fields[0, 0]
    for step_index in range(STEPS):
        base_square = jnp.sum(base_state * base_state, axis=(1, 2))
        extra_square = jnp.sum(extra_state * extra_state, axis=(0, 1))
        tile_total, helper_total = partner_totals(base_square[:, None, :], extra_square[None, :])
        factor = spring_factor(tile_total[:, 0, :], counts[:, None])
        helper_factor = spring_factor(helper_total[0], float(ALL_FIELDS))
        base_state = advance(base_state, tile_grad, factor, base_noise[0, 0, :, step_index])
        extra_state = advance(
            extra_state, helper_grad, helper_factor, extra_noise[0, 0, step_index]
        )
    moment_total, helper_moments = partner_totals(moments(base_state), moments(extra_state))
    stress = polymer_stress(moment_total, counts[:, None, None])
    return (base_state[None, None], extra_state[None, None], stress[None, None])


def solution(mesh):
    in_specs = (
        P(None, "gx", "gy", None),
        P("gx", "gy", None),
        P("gx", "gy", None),
        P("gx", None),
        P("gx", "gy", None, None, None, None),
        P("gx", "gy", None, None, None),
        P("gx", "gy", None, None, None, None, None),
        P("gx", "gy", None, None, None, None),
    )
    out_specs = (
        P("gx", "gy", None, None, None, None),
        P("gx", "gy", None, None, None),
        P("gx", "gy", None, None, None),
    )
    return jax.shard_map(
        per_device, mesh=mesh, in_specs=in_specs, out_specs=out_specs, check_vma=False
    )
```

profile of v0, /device:TPU:32, one launch (start us, length us, event | category | flops | bytes accessed | tf_op | source)
XLA Modules:
  0.0 229.3 jit_solution(16822083039907746352)
XLA Ops:
  0.6 0.9 fusion.76
  1.5 1.9 collective-permute-start.1
  3.4 3.6 %collective-permute-start = (f32[3,1,8,128]{3,2,1,0:T(8,128)S(1)}, f32[3,1,8,128]{3,2,1,0:T(8,128)S(1)}, u32[]{:S(2)}, u32[]{:S(2)}) collective-permute-start(f32[3,1,8,128]{3,2,1,0:T(8,128)S(1)} %get-tuple-element.56), channel_id=1, source_target_pairs={{16,0},{32,16},{48,32},{64,48},{80,64},{96,80},{112,96},{17,1},{33... | collective-permute-start | bytes 36872 | tf_op jit(solution)/shard_map/ppermute | solution.py:28
  7.1 1.3 fusion.73
  8.4 0.7 compare_convert_fusion.1
  9.1 1.3 compare_convert_fusion.2
  10.4 0.8 compare_convert_fusion
  11.2 2.3 %multiply_reduce_fusion.2 = f32[8,1024]{1,0:T(8,128)S(1)} fusion(f32[1,1,8,3,32,1024]{5,4,3,2,1,0:T(8,128)} %param.13), kind=kLoop, calls=%fused_computation.6 | loop fusion | flops 1564672 | bytes 3178496 | tf_op jit(solution)/shard_map/reduce_sum | solution.py:141
  14.7 24.3 %all-gather.3 = f32[16,4,1025]{2,1,0:T(4,128)S(1)} all-gather(f32[1,4,1025]{2,1,0:T(4,128)S(1)} %fusion.68), channel_id=1, replica_groups=mesh['gx'=8,'gy'=16] {'gy'}, dimensions={0}, use_global_device_ids=true | all-gather | bytes 278800 | tf_op jit(solution)/shard_map/all_gather | solution.py:38
  40.0 4.2 %fusion.74 = (bf16[1,1,8,1,3,32,1024]{6,5,4,3,2,1,0:T(8,128)(2,1)}, bf16[1,1,8,1,3,32,1024]{6,5,4,3,2,1,0:T(8,128)(2,1)}) fusion(bf16[1,1,8,2,3,32,1024]{6,5,4,3,2,1,0:T(8,128)(2,1)} %param.15), kind=kLoop, calls=%fused_computation.231 | loop fusion | bytes 6291456 | tf_op jit(solution)/shard_map/slice | solution.py:146
  45.6 0.8 reshape.2434
  46.5 1.3 collective-permute-start.2
  47.8 4.5 %collective-permute-start.3 = (f32[3,10,1,128]{3,2,1,0:T(1,128)S(1)}, f32[3,10,1,128]{3,2,1,0:T(1,128)S(1)}, u32[]{:S(2)}, u32[]{:S(2)}) collective-permute-start(f32[3,10,1,128]{3,2,1,0:T(1,128)S(1)} %get-tuple-element.52), channel_id=1, source_target_pairs={{0,1},{1,2},{2,3},{3,4},{4,5},{5,6},{6,7},{7,8},{8,9},{9,10},{10,1... | collective-permute-start | bytes 46088 | tf_op jit(solution)/shard_map/ppermute | solution.py:27
  52.4 25.1 %all-gather = f32[16384]{0:T(1024)S(1)} all-gather(f32[1024]{0:T(1024)S(1)} %multiply_reduce_fusion.3), channel_id=2, replica_groups=mesh['gx'=8,'gy'=16] {'gy'}, dimensions={0}, use_global_device_ids=true | all-gather | bytes 69632 | tf_op jit(solution)/shard_map/all_gather | solution.py:131
  77.5 0.6 mul.1495
  78.6 2.1 stack.98
  80.7 1.9 multiply_bitcast_fusion
  82.6 1.8 copy.62
  84.4 3.3 %reshape.2433 = f32[8,9,1024]{2,0,1:T(8,128)S(1)} reshape(f32[8,9,8,8,16]{4,3,2,0,1:T(8,128)} %copy.62) | data formatting | bytes 589824 | tf_op jit(solution)/shard_map/reshape | solution.py:107
  87.7 2.6 %multiply_reduce_fusion = f32[16,9,1024]{2,1,0:T(8,128)} fusion(f32[8,9,1024]{2,0,1:T(8,128)S(1)} %reshape.2433, f32[16,8]{1,0:T(8,128)S(1)} %compare_convert_fusion.1), kind=kLoop, calls=%fused_computation | loop fusion | flops 2211840 | bytes 885248 | tf_op jit(solution)/shard_map/reduce_sum | solution.py:123
  90.4 4.3 %all-to-all-start = ((f32[16,9,1024]{2,1,0:T(8,128)}), f32[16,9,1024]{2,1,0:T(8,128)}, u32[]{:S(2)}, u32[]{:S(2)}) async-start(f32[16,9,1024]{2,1,0:T(8,128)} %multiply_reduce_fusion), calls=%async_computation | async-start | bytes 2097152 | tf_op jit(solution)/shard_map/all_to_all | solution.py:124
  94.7 4.1 %copy_bitcast_fusion.1 = (bf16[8,3,32,1024]{3,2,0,1:T(8,128)(2,1)}, bf16[8,3,32,1024]{3,2,0,1:T(8,128)(2,1)}) fusion(bf16[1,1,8,1,3,32,1024]{6,5,4,3,2,1,0:T(8,128)(2,1)} %get-tuple-element.41, bf16[1,1,8,1,3,32,1024]{6,5,4,3,2,1,0:T(8,128)(2,1)} %get-tuple-element.42), kind=kLoop, calls=%fused_computation.12 | loop fusion | bytes 6291456 | tf_op jit(solution)/shard_map/squeeze | solution.py:146
  98.8 0.7 slice_bitcast_fusion.9
  99.5 8.2 %all-to-all-done = f32[16,9,1024]{2,1,0:T(8,128)} async-done(((f32[16,9,1024]{2,1,0:T(8,128)}), f32[16,9,1024]{2,1,0:T(8,128)}, u32[]{:S(2)}, u32[]{:S(2)}) %all-to-all-start) | async-done | bytes 589856 | tf_op jit(solution)/shard_map/all_to_all | solution.py:124
  107.6 1.3 reduce_sum.250
  109.0 2.4 %bitcast_add_fusion.17 = f32[1,224,1024]{2,1,0:T(8,128)S(1)} fusion(f32[1,1,3,224,1024]{4,3,2,1,0:T(8,128)} %param.14, f32[1024]{0:T(1024)S(1)} %bitcast.430, f32[1024]{0:T(1024)S(1)} %bitcast.422, f32[1024]{0:T(1024)S(1)} %bitcast.426, f32[1024]{0:T(1024)} %divide_multiply_fusion.3, bf16[1,1,2,3,224,1024]{5,4,3,2,1,0:T(8,128)(2,1)} %param.16), kind=kLoop, calls=%fused_computation.101 | loop fusion | flops 2752512 | bytes 4145152 | tf_op jit(solution)/shard_map/add | solution.py:65
  111.7 1.9 bitcast_add_fusion.19
  113.7 0.9 copy-done.8
  115.5 23.9 %all-gather.1 = f32[16384]{0:T(1024)} all-gather(f32[1024]{0:T(1024)S(1)} %fusion.1), channel_id=3, replica_groups=mesh['gx'=8,'gy'=16] {'gy'}, dimensions={0}, use_global_device_ids=true | all-gather | bytes 69632 | tf_op jit(solution)/shard_map/all_gather | solution.py:131
  139.4 1.5 mul.1583
  140.9 1.2 multiply_reduce_fusion.16
  142.2 0.7 divide_multiply_fusion.1
  142.9 1.5 fusion.17
  144.5 0.9 fusion.19
  146.1 0.7 copy-done.3
  146.8 1.5 fusion.16
  148.3 2.3 add_bitcast_fusion.1
  150.7 3.2 %bitcast_add_fusion.2 = (f32[8,32,1024]{2,1,0:T(8,128)}, f32[8,32,1024]{2,1,0:T(8,128)}, f32[8,32,1024]{2,1,0:T(8,128)}, f32[8,32,1024]{2,1,0:T(8,128)}) fusion(f32[8,1024]{1,0:T(8,128)S(1)} %divide_multiply_fusion, f32[8,1024]{1,0:T(8,128)S(1)} %copy-done.25, f32[8,1024]{1,0:T(8,128)S(1)} %copy-done.26, f32[8,1024]{1,0:T(8,128)S(1)} %copy-done.24, ...), kind=kLoop, calls=%fused_computation.17 | loop fusion | flops 12582912 | bytes 9797632 | tf_op jit(solution)/shard_map/add | solution.py:65
  153.9 22.9 %all-gather.4 = f32[16,4,1025]{2,1,0:T(4,128)S(1)} all-gather(f32[1,4,1025]{2,1,0:T(4,128)S(1)} %fusion.69), channel_id=1, replica_groups=mesh['gx'=8,'gy'=16] {'gy'}, dimensions={0}, use_global_device_ids=true | all-gather | bytes 278800 | tf_op jit(solution)/shard_map/all_gather | solution.py:38
  177.1 0.7 divide_multiply_fusion.2
  177.8 4.7 %bitcast_add_fusion.16 = (f32[1,224,1024]{2,1,0:T(8,128)}, f32[1,224,1024]{2,1,0:T(8,128)}, f32[1,224,1024]{2,1,0:T(8,128)}) fusion(f32[1,224,1024]{2,1,0:T(8,128)} %copy-done.8, f32[1,224,1024]{2,1,0:T(8,128)} %copy-done.10, f32[1,224,1024]{2,1,0:T(8,128)} %copy-done.9, f32[1024]{0:T(1024)S(1)} %divide_multiply_fusion.2, f32[1024]{0:T(1024)} %bitcast.438, ...), kind=kLoop, calls=%fused_computation.100 | loop fusion | flops 8257536 | bytes 6922240 | tf_op jit(solution)/shard_map/add | solution.py:65
  182.6 1.4 bitcast_add_fusion.9
  184.9 0.9 bitcast_add_fusion
  186.1 0.8 multiply_reduce_fusion.4
  186.9 0.6 bitcast_dynamic-update-slice_fusion.5
  187.5 0.6 copy.75
  188.1 0.6 copy.76
  188.8 0.6 copy.77
  189.4 0.6 copy.78
  190.0 0.6 copy.79
  190.7 0.6 stack.122
  191.3 0.7 bitcast_add_fusion.7
  192.6 22.6 %all-gather.5 = f32[16,6,1024]{2,1,0:T(8,128)S(1)} all-gather(f32[1,6,1024]{2,1,0:T(8,128)S(1)} %bitcast.409), channel_id=4, replica_groups=mesh['gx'=8,'gy'=16] {'gy'}, dimensions={0}, use_global_device_ids=true | all-gather | bytes 417792 | tf_op jit(solution)/shard_map/all_gather | solution.py:131
  216.1 1.4 bitcast_dynamic-update-slice_fusion.4
  217.4 0.6 bitcast_dynamic-update-slice_fusion.3
  218.1 0.6 bitcast_dynamic-update-slice_fusion.2
  218.7 0.6 bitcast_dynamic-update-slice_fusion.1
  219.9 1.1 fusion.55
  221.0 1.8 stack.123
  222.8 1.1 fusion.54
  223.9 0.8 copy.80
  224.7 1.9 maximum_bitcast_fusion
  226.9 0.7 copy-done.20
  227.5 1.7 maximum_bitcast_fusion.1
  (154 shorter events, 9.2 us)
Async XLA Ops:
  0.6 12.9 %copy-start = (f32[1,1,3,224,1024]{4,3,2,1,0:T(8,128)S(1)}, f32[1,1,3,224,1024]{4,3,2,1,0:T(8,128)}, u32[]{:S(2)}) copy-start(f32[1,1,3,224,1024]{4,3,2,1,0:T(8,128)} %param.14) | copy-start | bytes 8257540
  1.5 44.9 %collective-permute-start.1 = (f32[3,1,8,128]{3,2,1,0:T(8,128)S(1)}, f32[3,1,8,128]{3,2,1,0:T(8,128)S(1)}, u32[]{:S(2)}, u32[]{:S(2)}) collective-permute-start(f32[3,1,8,128]{3,2,1,0:T(8,128)S(1)} %get-tuple-element.57), channel_id=1, source_target_pairs={{0,16},{16,32},{32,48},{48,64},{64,80},{80,96},{96,112},{1,17},{17... | collective-permute-start | bytes 36872 | tf_op jit(solution)/shard_map/ppermute | solution.py:27
  3.4 43.0 %collective-permute-start = (f32[3,1,8,128]{3,2,1,0:T(8,128)S(1)}, f32[3,1,8,128]{3,2,1,0:T(8,128)S(1)}, u32[]{:S(2)}, u32[]{:S(2)}) collective-permute-start(f32[3,1,8,128]{3,2,1,0:T(8,128)S(1)} %get-tuple-element.56), channel_id=1, source_target_pairs={{16,0},{32,16},{48,32},{64,48},{80,64},{96,80},{112,96},{17,1},{33... | collective-permute-start | bytes 36872 | tf_op jit(solution)/shard_map/ppermute | solution.py:28
  11.2 2.6 %copy-start.55 = (s32[1,1,8]{2,1,0:T(1,128)S(1)}, s32[1,1,8]{2,1,0:T(1,128)}, u32[]{:S(2)}) copy-start(s32[1,1,8]{2,1,0:T(1,128)} %param.11) | copy-start | bytes 100
  13.5 30.7 %copy-start.27 = (f32[8,1024]{1,0:T(8,128)}, f32[8,1024]{1,0:T(8,128)S(1)}, u32[]{:S(2)}) copy-start(f32[8,1024]{1,0:T(8,128)S(1)} %multiply_reduce_fusion.2) | copy-start | bytes 98308
  14.0 0.6 copy-start.50
  14.6 29.7 %copy-start.48 = (f32[4,1]{1,0:T(4,128)}, f32[4,1]{1,0:T(4,128)S(1)}, u32[]{:S(2)}) copy-start(f32[4,1]{1,0:T(4,128)S(1)} %copy.65) | copy-start | bytes 52
  40.0 5.4 %copy-start.6 = (f32[1,1,8,3,32,1024]{5,4,3,2,1,0:T(8,128)S(1)}, f32[1,1,8,3,32,1024]{5,4,3,2,1,0:T(8,128)}, u32[]{:S(2)}) copy-start(f32[1,1,8,3,32,1024]{5,4,3,2,1,0:T(8,128)} %param.13) | copy-start | bytes 9437188
  45.4 1.1 copy-start.31
  46.5 31.6 %collective-permute-start.2 = (f32[3,10,1,128]{3,2,1,0:T(1,128)S(1)}, f32[3,10,1,128]{3,2,1,0:T(1,128)S(1)}, u32[]{:S(2)}, u32[]{:S(2)}) collective-permute-start(f32[3,10,1,128]{3,2,1,0:T(1,128)S(1)} %get-tuple-element.53), channel_id=1, source_target_pairs={{1,0},{2,1},{3,2},{4,3},{5,4},{6,5},{7,6},{8,7},{9,8},{10,9},{11,1... | collective-permute-start | bytes 46088 | tf_op jit(solution)/shard_map/ppermute | solution.py:28
  47.8 30.3 %collective-permute-start.3 = (f32[3,10,1,128]{3,2,1,0:T(1,128)S(1)}, f32[3,10,1,128]{3,2,1,0:T(1,128)S(1)}, u32[]{:S(2)}, u32[]{:S(2)}) collective-permute-start(f32[3,10,1,128]{3,2,1,0:T(1,128)S(1)} %get-tuple-element.52), channel_id=1, source_target_pairs={{0,1},{1,2},{2,3},{3,4},{4,5},{5,6},{6,7},{7,8},{8,9},{9,10},{10,1... | collective-permute-start | bytes 46088 | tf_op jit(solution)/shard_map/ppermute | solution.py:27
  90.4 17.3 %all-to-all-start = ((f32[16,9,1024]{2,1,0:T(8,128)}), f32[16,9,1024]{2,1,0:T(8,128)}, u32[]{:S(2)}, u32[]{:S(2)}) async-start(f32[16,9,1024]{2,1,0:T(8,128)} %multiply_reduce_fusion), calls=%async_computation | async-start | bytes 2097152 | tf_op jit(solution)/shard_map/all_to_all | solution.py:124
  99.5 11.9 %copy-start.38 = (f32[1024]{0:T(1024)S(1)}, f32[1024]{0:T(1024)}, u32[]{:S(2)}) copy-start(f32[1024]{0:T(1024)} %divide_multiply_fusion.3) | copy-start | bytes 12292
  108.9 2.8 %copy-start.1 = (f32[1,1,3,224,1024]{4,3,2,1,0:T(8,128)S(1)}, f32[1,1,3,224,1024]{4,3,2,1,0:T(8,128)}, u32[]{:S(2)}) copy-start(f32[1,1,3,224,1024]{4,3,2,1,0:T(8,128)} %param.14) | copy-start | bytes 8257540
  109.0 4.7 %copy-start.32 = (f32[1,1024]{1,0:T(1,128)}, f32[1,1024]{1,0:T(1,128)S(1)}, u32[]{:S(2)}) copy-start(f32[1,1024]{1,0:T(1,128)S(1)} %get-tuple-element.60) | copy-start | bytes 12292
  109.0 4.7 %copy-start.35 = (f32[1,1024]{1,0:T(1,128)}, f32[1,1024]{1,0:T(1,128)S(1)}, u32[]{:S(2)}) copy-start(f32[1,1024]{1,0:T(1,128)S(1)} %get-tuple-element.66) | copy-start | bytes 12292
  109.0 4.7 %copy-start.40 = (f32[1,1024]{1,0:T(1,128)}, f32[1,1024]{1,0:T(1,128)S(1)}, u32[]{:S(2)}) copy-start(f32[1,1024]{1,0:T(1,128)S(1)} %get-tuple-element.58) | copy-start | bytes 12292
  109.0 4.7 %copy-start.42 = (f32[1,1024]{1,0:T(1,128)}, f32[1,1024]{1,0:T(1,128)S(1)}, u32[]{:S(2)}) copy-start(f32[1,1024]{1,0:T(1,128)S(1)} %get-tuple-element.64) | copy-start | bytes 12292
  109.0 4.7 %copy-start.44 = (f32[1,1024]{1,0:T(1,128)}, f32[1,1024]{1,0:T(1,128)S(1)}, u32[]{:S(2)}) copy-start(f32[1,1024]{1,0:T(1,128)S(1)} %get-tuple-element.65) | copy-start | bytes 12292
  111.4 2.3 %copy-start.10 = (f32[1,224,1024]{2,1,0:T(8,128)}, f32[1,224,1024]{2,1,0:T(8,128)S(1)}, u32[]{:S(2)}) copy-start(f32[1,224,1024]{2,1,0:T(8,128)S(1)} %bitcast_add_fusion.17) | copy-start | bytes 2752516
  113.7 1.0 copy-start.8
  113.7 1.2 copy-start.9
  113.7 27.2 %copy-start.30 = (f32[16,1024]{1,0:T(8,128)S(1)}, f32[16,1024]{1,0:T(8,128)}, u32[]{:S(2)}) copy-start(f32[16,1024]{1,0:T(8,128)} %mul.1495) | copy-start | bytes 196612
  113.7 28.5 %copy-start.28 = (f32[8,1024]{1,0:T(8,128)S(1)}, f32[8,1024]{1,0:T(8,128)}, u32[]{:S(2)}) copy-start(f32[8,1024]{1,0:T(8,128)} %copy-done.27) | copy-start | bytes 98308
  114.9 0.6 copy-start.47
  115.5 28.9 %copy-start.21 = (f32[8,1024]{1,0:T(8,128)S(1)}, f32[8,1024]{1,0:T(8,128)}, u32[]{:S(2)}) copy-start(f32[8,1024]{1,0:T(8,128)} %get-tuple-element.47) | copy-start | bytes 98308
  115.5 28.9 %copy-start.22 = (f32[8,1024]{1,0:T(8,128)S(1)}, f32[8,1024]{1,0:T(8,128)}, u32[]{:S(2)}) copy-start(f32[8,1024]{1,0:T(8,128)} %get-tuple-element.48) | copy-start | bytes 98308
  115.5 28.9 %copy-start.23 = (f32[8,1024]{1,0:T(8,128)S(1)}, f32[8,1024]{1,0:T(8,128)}, u32[]{:S(2)}) copy-start(f32[8,1024]{1,0:T(8,128)} %get-tuple-element.49) | copy-start | bytes 98308
  115.5 28.9 %copy-start.24 = (f32[8,1024]{1,0:T(8,128)S(1)}, f32[8,1024]{1,0:T(8,128)}, u32[]{:S(2)}) copy-start(f32[8,1024]{1,0:T(8,128)} %get-tuple-element.43) | copy-start | bytes 98308
  115.5 28.9 %copy-start.25 = (f32[8,1024]{1,0:T(8,128)S(1)}, f32[8,1024]{1,0:T(8,128)}, u32[]{:S(2)}) copy-start(f32[8,1024]{1,0:T(8,128)} %get-tuple-element.50) | copy-start | bytes 98308
  115.5 28.9 %copy-start.26 = (f32[8,1024]{1,0:T(8,128)S(1)}, f32[8,1024]{1,0:T(8,128)}, u32[]{:S(2)}) copy-start(f32[8,1024]{1,0:T(8,128)} %get-tuple-element.51) | copy-start | bytes 98308
  140.9 3.6 %copy-start.5 = (bf16[8,3,32,1024]{3,2,0,1:T(8,128)(2,1)S(1)}, bf16[8,3,32,1024]{3,2,0,1:T(8,128)(2,1)}, u32[]{:S(2)}) copy-start(bf16[8,3,32,1024]{3,2,0,1:T(8,128)(2,1)} %get-tuple-element.72) | copy-start | bytes 4718596
  145.4 0.6 copy-start.52
  145.4 1.4 copy-start.3
  148.3 2.3 copy-start.51
  150.7 3.2 %copy-start.49 = (f32[4,1]{1,0:T(4,128)S(1)}, f32[4,1]{1,0:T(4,128)}, u32[]{:S(2)}) copy-start(f32[4,1]{1,0:T(4,128)} %copy-done.48) | copy-start | bytes 52
  150.7 27.1 %copy-start.33 = (f32[1,1024]{1,0:T(1,128)S(1)}, f32[1,1024]{1,0:T(1,128)}, u32[]{:S(2)}) copy-start(f32[1,1024]{1,0:T(1,128)} %copy-done.32) | copy-start | bytes 12292
  150.7 27.1 %copy-start.36 = (f32[1,1024]{1,0:T(1,128)S(1)}, f32[1,1024]{1,0:T(1,128)}, u32[]{:S(2)}) copy-start(f32[1,1024]{1,0:T(1,128)} %copy-done.35) | copy-start | bytes 12292
  150.7 27.1 %copy-start.41 = (f32[1,1024]{1,0:T(1,128)S(1)}, f32[1,1024]{1,0:T(1,128)}, u32[]{:S(2)}) copy-start(f32[1,1024]{1,0:T(1,128)} %copy-done.40) | copy-start | bytes 12292
  177.8 4.7 %copy-start.2 = (f32[1,1,3,224,1024]{4,3,2,1,0:T(8,128)S(1)}, f32[1,1,3,224,1024]{4,3,2,1,0:T(8,128)}, u32[]{:S(2)}) copy-start(f32[1,1,3,224,1024]{4,3,2,1,0:T(8,128)} %param.14) | copy-start | bytes 8257540
  177.8 4.7 %copy-start.7 = (bf16[1,1,2,3,224,1024]{5,4,3,2,1,0:T(8,128)(2,1)S(1)}, bf16[1,1,2,3,224,1024]{5,4,3,2,1,0:T(8,128)(2,1)}, u32[]{:S(2)}) copy-start(bf16[1,1,2,3,224,1024]{5,4,3,2,1,0:T(8,128)(2,1)} %param.16) | copy-start | bytes 8257540
  177.8 4.7 %copy-start.39 = (f32[1024]{0:T(1024)S(1)}, f32[1024]{0:T(1024)}, u32[]{:S(2)}) copy-start(f32[1024]{0:T(1024)} %divide_multiply_fusion.3) | copy-start | bytes 12292
  177.8 4.7 %copy-start.43 = (f32[1,1024]{1,0:T(1,128)S(1)}, f32[1,1024]{1,0:T(1,128)}, u32[]{:S(2)}) copy-start(f32[1,1024]{1,0:T(1,128)} %copy-done.42) | copy-start | bytes 12292
  177.8 4.7 %copy-start.45 = (f32[1,1024]{1,0:T(1,128)S(1)}, f32[1,1024]{1,0:T(1,128)}, u32[]{:S(2)}) copy-start(f32[1,1024]{1,0:T(1,128)} %copy-done.44) | copy-start | bytes 12292
  182.5 1.5 copy-start.4
  182.5 1.7 copy-start.12
  182.6 2.0 copy-start.13
  182.6 2.3 %copy-start.14 = (f32[8,32,1024]{2,1,0:T(8,128)S(1)}, f32[8,32,1024]{2,1,0:T(8,128)}, u32[]{:S(2)}) copy-start(f32[8,32,1024]{2,1,0:T(8,128)} %get-tuple-element.27) | copy-start | bytes 3145732
  184.9 1.2 copy-start.11
  185.8 5.5 %copy-start.34 = (f32[1,1024]{1,0:T(1,128)S(1)}, f32[1,1024]{1,0:T(1,128)}, u32[]{:S(2)}) copy-start(f32[1,1024]{1,0:T(1,128)} %copy-done.32) | copy-start | bytes 12292
  185.8 5.5 %copy-start.37 = (f32[1,1024]{1,0:T(1,128)S(1)}, f32[1,1024]{1,0:T(1,128)}, u32[]{:S(2)}) copy-start(f32[1,1024]{1,0:T(1,128)} %copy-done.35) | copy-start | bytes 12292
  186.8 5.2 %copy-start.29 = (f32[8,1024]{1,0:T(8,128)}, f32[8,1024]{1,0:T(8,128)S(1)}, u32[]{:S(2)}) copy-start(f32[8,1024]{1,0:T(8,128)S(1)} %get-tuple-element.11) | copy-start | bytes 98308
  192.0 23.4 %copy-start.46 = (f32[8,16]{1,0:T(8,128)S(1)}, f32[8,16]{1,0:T(8,128)}, u32[]{:S(2)}) copy-start(f32[8,16]{1,0:T(8,128)} %compare_convert_fusion.2) | copy-start | bytes 1540
  192.0 27.9 %copy-start.53 = (f32[8]{0:T(128)S(1)}, f32[8]{0:T(128)}, u32[]{:S(2)}) copy-start(f32[8]{0:T(128)} %convert_bitcast_fusion) | copy-start | bytes 100
  192.1 30.7 %copy-start.54 = (f32[6]{0:T(128)S(1)}, f32[6]{0:T(128)}, u32[]{:S(2)}) copy-start(f32[6]{0:T(128)} %constant.69) | copy-start | bytes 76
  192.5 32.2 %copy-start.15 = (f32[8,1,32,1024]{3,2,1,0:T(8,128)S(1)}, f32[8,1,32,1024]{3,2,1,0:T(8,128)}, u32[]{:S(2)}) copy-start(f32[8,1,32,1024]{3,2,1,0:T(8,128)} %fusion.16) | copy-start | bytes 3145732
  192.5 32.2 %copy-start.16 = (f32[8,1,32,1024]{3,2,1,0:T(8,128)S(1)}, f32[8,1,32,1024]{3,2,1,0:T(8,128)}, u32[]{:S(2)}) copy-start(f32[8,1,32,1024]{3,2,1,0:T(8,128)} %get-tuple-element.37) | copy-start | bytes 3145732
  192.5 32.2 %copy-start.17 = (f32[8,1,32,1024]{3,2,1,0:T(8,128)S(1)}, f32[8,1,32,1024]{3,2,1,0:T(8,128)}, u32[]{:S(2)}) copy-start(f32[8,1,32,1024]{3,2,1,0:T(8,128)} %get-tuple-element.38) | copy-start | bytes 3145732
  224.7 1.9 copy-start.18
  224.7 2.2 copy-start.19
  224.7 2.9 %copy-start.20 = (f32[1,224,1024]{2,1,0:T(8,128)S(1)}, f32[1,224,1024]{2,1,0:T(8,128)}, u32[]{:S(2)}) copy-start(f32[1,224,1024]{2,1,0:T(8,128)} %get-tuple-element.32) | copy-start | bytes 2752516
where the time goes:
time: 231 us; the launch traced here: 229 us
  blocking collectives  119 us (52%)
  other arithmetic  47.3 us (20%)
  local copies, waits for them, and re-layouts  37.2 us (16%)
  starting transfers between devices  15.7 us (7%)
  waiting for transfers between devices  8.16 us (4%)
    all_gather x3, blocking collectives, partner_totals(): lax.all_gather(extra_rows[None], 'gy', axis=0, tiled=True)  71.6 us
    all_gather x2, blocking collectives, in_one_piece(): out = lax.all_gather(both, axis, axis=dim, tiled=True)  47.2 us
    add x11, other arithmetic, advance(): current + time_step * (drift - relax * current)  21.4 us
    unnamed x122, local copies, waits for them, and re-layouts  10.5 us
    all_to_all x1, waiting for transfers between devices, per_device(): lax.all_to_all(outgoing, 'gy', split_axis=0, concat_axis=0, tiled=True)  8.15 us
    ppermute x2, starting transfers between devices, extended(): before = lax.ppermute(last, axis, up)  6.46 us
    another operation x9, local copies, waits for them, and re-layouts, moments(): jnp.stack([jnp.sum(state[..., first_axis, :, :] * state[..., second_axis,...  6.28 us
    ppermute x2, starting transfers between devices, extended(): after = lax.ppermute(leading, axis, down)  4.93 us
  transfers between devices with their start and end apart: 5, of which 1 were waited for; matrix products, arithmetic and copies ran while one was open for 8% of the time, Pallas kernels for 0%

commit v1 on v0

v1 whole, which is shorter than its diff:
```python
import functools

import jax
import jax.numpy as jnp
from jax import lax
from jax.experimental import pallas as pl
from jax.experimental.pallas import tpu as pltpu
from jax.sharding import PartitionSpec as P

MESH = pl.DeviceIdType.MESH
F32 = jnp.float32

STEPS = 2
TILES = 8
CELLS = 1024
LANES = 128
CHUNKS = CELLS // LANES
BASE = 32
EXTRA = 224
GROUP = 32

time_step = 0.05
weissenberg = 0.25
max_extension = 50.0
noise_scale = (time_step / weissenberg) ** 0.5
relax_scale = time_step * (0.5 / weissenberg)
component_pairs = ((0, 0), (1, 1), (2, 2), (0, 1), (0, 2), (1, 2))


def wide(row):
    return jnp.broadcast_to(row, (GROUP, LANES))


def matrix(grad_row, relax_row):
    keep = wide(1.0 - relax_row)
    rows = []
    for a in range(3):
        row = [wide(grad_row(3 * a + b)) for b in range(3)]
        row[a] = row[a] + keep
        rows.append(row)
    return rows


def advance(mat, state, noise):
    return [
        mat[a][0] * state[0]
        + mat[a][1] * state[1]
        + mat[a][2] * state[2]
        + noise_scale * noise[a].astype(F32)
        for a in range(3)
    ]


def fold(block):
    out = block[:8]
    for k in range(1, block.shape[0] // 8):
        out = out + block[8 * k : 8 * k + 8]
    return out


def squares(state):
    return fold(state[0] * state[0] + state[1] * state[1] + state[2] * state[2])


def products(state):
    return [fold(state[a] * state[b]) for a, b in component_pairs]


def row_sum(block):
    return jnp.sum(block, axis=0, keepdims=True)


def kernel(
    n_gx,
    n_gy,
    counts,
    helper,
    vel_hbm,
    wall_hbm,
    base_hbm,
    extra_hbm,
    base_noise_hbm,
    extra_noise_hbm,
    base,
    extra,
    stress,
    vel,
    wall,
    base_noise,
    extra_noise,
    y_edge,
    x_halo,
    y_halo,
    tile_grad,
    helper_grad,
    grad_send,
    grad_recv,
    own_sum,
    extra_sum,
    sum_send,
    first_recv,
    second_recv,
    relax,
    helper_relax,
    own_moment,
    moment_recv,
    in_sem,
    tile_sem,
    halo_send_sem,
    halo_recv_sem,
    grad_send_sem,
    grad_recv_sem,
    sum_send_sem,
    sum_recv_sem,
    moment_send_sem,
    moment_recv_sem,
):
    gx = lax.axis_index("gx")
    gy = lax.axis_index("gy")
    up_x, down_x = lax.rem(gx + 1, n_gx), lax.rem(gx + n_gx - 1, n_gx)
    up_y, down_y = lax.rem(gy + 1, n_gy), lax.rem(gy + n_gy - 1, n_gy)

    vel_copy = pltpu.make_async_copy(vel_hbm, vel, in_sem.at[0])
    wall_copy = pltpu.make_async_copy(wall_hbm, wall, in_sem.at[1])
    extra_copy = pltpu.make_async_copy(extra_hbm, extra, in_sem.at[2])
    base_copies = [
        pltpu.make_async_copy(base_hbm.at[t], base.at[t], tile_sem.at[t]) for t in range(TILES)
    ]
    base_noise_copies = [
        pltpu.make_async_copy(base_noise_hbm.at[:, s], base_noise.at[s], in_sem.at[3 + s])
        for s in range(STEPS)
    ]
    extra_noise_copies = [
        pltpu.make_async_copy(extra_noise_hbm.at[s], extra_noise.at[s], in_sem.at[5 + s])
        for s in range(STEPS)
    ]
    vel_copy.start()
    wall_copy.start()
    for copy in base_copies:
        copy.start()
    extra_copy.start()
    for s in range(STEPS):
        base_noise_copies[s].start()
        extra_noise_copies[s].start()

    barrier = pltpu.get_barrier_semaphore()
    for k in range(1, n_gy):
        peer = lax.rem(gy + k, n_gy)
        pl.semaphore_signal(barrier, inc=1, device_id=(gx, peer), device_id_type=MESH)
    for peer in (up_x, down_x):
        pl.semaphore_signal(barrier, inc=1, device_id=(peer, gy), device_id_type=MESH)

    my_tile = helper[gy]
    my_slot = lax.rem(gy - my_tile // TILES + n_gy, n_gy)
    slot_of, found = [], []
    for t in range(TILES):
        slot, hit = jnp.int32(0), jnp.int32(0)
        for h in range(n_gy):
            match = helper[h] == gy * TILES + t
            slot = jnp.where(match, lax.rem(gy - h + n_gy, n_gy), slot)
            hit = jnp.where(match, 1, hit)
        slot_of.append(slot)
        found.append(hit)

    vel_copy.wait()
    for c in range(3):
        y_edge[0, c] = vel[c, :, 7, :]
        y_edge[1, c] = vel[c, :, 0, :]
    pl.semaphore_wait(barrier, n_gy + 1)

    halo_copies = [
        pltpu.make_async_remote_copy(
            src_ref=src,
            dst_ref=dst,
            send_sem=halo_send_sem.at[i],
            recv_sem=halo_recv_sem.at[i],
            device_id=device,
            device_id_type=MESH,
        )
        for i, (src, dst, device) in enumerate(
            (
                (vel.at[:, 7], x_halo.at[0], (up_x, gy)),
                (vel.at[:, 0], x_halo.at[1], (down_x, gy)),
                (y_edge.at[0], y_halo.at[0], (gx, up_y)),
                (y_edge.at[1], y_halo.at[1], (gx, down_y)),
            )
        )
    ]
    for copy in halo_copies:
        copy.start()

    def peer_copies(src_of, dst_of, send_sem, recv_sem):
        return [
            pltpu.make_async_remote_copy(
                src_ref=src_of(k),
                dst_ref=dst_of(k),
                send_sem=send_sem(k),
                recv_sem=recv_sem(k),
                device_id=(gx, lax.rem(gy + k, n_gy)),
                device_id_type=MESH,
            )
            for k in range(1, n_gy)
        ]

    sum_recv = (first_recv, second_recv)

    def sum_exchange(r):
        @pl.loop(0, n_gy)
        def _(k):
            tile = lax.rem(helper[lax.rem(gy + k, n_gy)], TILES)
            sum_send[r, k, 0] = own_sum[tile]
            sum_send[r, k, 1] = extra_sum[...]

        copies = peer_copies(
            lambda k: sum_send.at[r, k],
            lambda k: sum_recv[r].at[k],
            lambda k: sum_send_sem.at[r, k],
            lambda k: sum_recv_sem.at[r, k],
        )
        for copy in copies:
            copy.start()
        sum_recv[r][0] = sum_send[r, 0]
        return copies

    def factors(r, copies):
        for copy in copies:
            copy.wait_recv()
        for t in range(TILES):
            count = jnp.full((CHUNKS, LANES), counts[t], jnp.int32).astype(F32)
            total = own_sum[t] + jnp.where(found[t] == 1, sum_recv[r][slot_of[t], 1], 0.0)
            relax[t] = relax_scale * (1.0 / (1.0 - total / count / max_extension))
        total = extra_sum[...] + sum_recv[r][my_slot, 0]
        helper_relax[...] = relax_scale * (1.0 / (1.0 - total / 256.0 / max_extension))

    for copy in base_copies:
        copy.wait()

    @pl.loop(0, TILES)
    def _(t):
        for x in range(CHUNKS):
            lanes = pl.ds(x * LANES, LANES)
            state = [base[t, c, :, lanes] for c in range(3)]
            own_sum[t, pl.ds(x, 1), :] = row_sum(squares(state))

    extra_copy.wait()

    @pl.loop(0, CHUNKS)
    def _(x):
        lanes = pl.ds(pl.multiple_of(x * LANES, LANES), LANES)
        total = jnp.zeros((8, LANES), F32)
        for f in range(EXTRA // GROUP):
            fields = pl.ds(f * GROUP, GROUP)
            total = total + squares([extra[c, fields, lanes] for c in range(3)])
        extra_sum[pl.ds(x, 1), :] = row_sum(total)

    first_sums = sum_exchange(0)

    wall_copy.wait()
    for copy in halo_copies:
        copy.wait_recv()
    sub = lax.broadcasted_iota(jnp.int32, (8, LANES), 0)
    lane = lax.broadcasted_iota(jnp.int32, (8, LANES), 1)
    block = lane // 16
    fluid = [
        jnp.where(wall[:, y, :] == 0, 0.5 * time_step, 0.0).astype(F32) for y in range(8)
    ]
    for a in range(3):
        here = [vel[a, :, y, :] for y in range(8)]
        low_y = jnp.where(gy > 0, y_halo[0, a], 0.0)
        high_y = jnp.where(gy < n_gy - 1, y_halo[1, a], 0.0)
        padded = [low_y] + here + [high_y]
        low_x = jnp.where(gx > 0, x_halo[0, a], 0.0)
        high_x = jnp.where(gx < n_gx - 1, x_halo[1, a], 0.0)
        columns = [[], [], []]
        for y in range(8):
            v = here[y]
            low = jnp.broadcast_to(low_x[y : y + 1], (8, LANES))
            high = jnp.broadcast_to(high_x[y : y + 1], (8, LANES))
            before = jnp.where(sub == 0, low, pltpu.roll(v, 1, 0))
            after = jnp.where(sub == 7, high, pltpu.roll(v, 7, 0))
            columns[0].append((after - before) * fluid[y])
            columns[1].append((padded[y + 2] - padded[y]) * fluid[y])
            before = jnp.where(lane == 0, 0.0, pltpu.roll(v, 1, 1))
            after = jnp.where(lane == LANES - 1, 0.0, pltpu.roll(v, LANES - 1, 1))
            columns[2].append((after - before) * fluid[y])
        for b in range(3):
            regs = columns[b]
            for bit in (1, 2, 4):
                upper = (block & bit) != 0
                new = list(regs)
                for i in range(8):
                    if i & bit:
                        continue
                    j = i | bit
                    new[i] = jnp.where(upper, pltpu.roll(regs[j], 16 * bit, 1), regs[i])
                    new[j] = jnp.where(upper, regs[j], pltpu.roll(regs[i], LANES - 16 * bit, 1))
                regs = new
            for t in range(TILES):
                tile_grad[t, 3 * a + b] = regs[t]

    @pl.loop(0, n_gy)
    def _(k):
        tile = lax.rem(helper[lax.rem(gy + k, n_gy)], TILES)
        grad_send[k] = tile_grad[tile]

    grad_copies = peer_copies(
        lambda k: grad_send.at[k],
        lambda k: grad_recv.at[k],
        lambda k: grad_send_sem.at[k],
        lambda k: grad_recv_sem.at[k],
    )
    for copy in grad_copies:
        copy.start()
    grad_recv[0] = grad_send[0]

    factors(0, first_sums)

    base_noise_copies[0].wait()

    @pl.loop(0, TILES)
    def _(t):
        for x in range(CHUNKS):
            lanes = pl.ds(x * LANES, LANES)
            mat = matrix(lambda c: tile_grad[t, c, pl.ds(x, 1), :], relax[t, pl.ds(x, 1), :])
            state = [base[t, c, :, lanes] for c in range(3)]
            noise = [base_noise[0, t, c, :, lanes] for c in range(3)]
            state = advance(mat, state, noise)
            for c in range(3):
                base[t, c, :, lanes] = state[c]
            own_sum[t, pl.ds(x, 1), :] = row_sum(squares(state))

    for copy in grad_copies:
        copy.wait_recv()
    helper_grad[...] = grad_recv[my_slot]
    extra_noise_copies[0].wait()

    @pl.loop(0, CHUNKS)
    def _(x):
        lanes = pl.ds(pl.multiple_of(x * LANES, LANES), LANES)
        mat = matrix(lambda c: helper_grad[c, pl.ds(x, 1), :], helper_relax[pl.ds(x, 1), :])
        total = jnp.zeros((8, LANES), F32)
        for f in range(EXTRA // GROUP):
            fields = pl.ds(f * GROUP, GROUP)
            state = [extra[c, fields, lanes] for c in range(3)]
            noise = [extra_noise[0, c, fields, lanes] for c in range(3)]
            state = advance(mat, state, noise)
            for c in range(3):
                extra[c, fields, lanes] = state[c]
            total = total + squares(state)
        extra_sum[pl.ds(x, 1), :] = row_sum(total)

    second_sums = sum_exchange(1)
    extra_noise_copies[1].wait()
    base_noise_copies[1].wait()
    factors(1, second_sums)

    @pl.loop(0, CHUNKS)
    def _(x):
        lanes = pl.ds(pl.multiple_of(x * LANES, LANES), LANES)
        mat = matrix(lambda c: helper_grad[c, pl.ds(x, 1), :], helper_relax[pl.ds(x, 1), :])
        totals = [jnp.zeros((8, LANES), F32) for _ in range(6)]
        for f in range(EXTRA // GROUP):
            fields = pl.ds(f * GROUP, GROUP)
            state = [extra[c, fields, lanes] for c in range(3)]
            noise = [extra_noise[1, c, fields, lanes] for c in range(3)]
            state = advance(mat, state, noise)
            for c in range(3):
                extra[c, fields, lanes] = state[c]
            totals = [u + v for u, v in zip(totals, products(state))]
        for m in range(6):
            moment_recv[0, m, pl.ds(x, 1), :] = row_sum(totals[m])

    moment_copies = peer_copies(
        lambda k: moment_recv.at[0],
        lambda k: moment_recv.at[k],
        lambda k: moment_send_sem.at[k],
        lambda k: moment_recv_sem.at[k],
    )
    for copy in moment_copies:
        copy.start()

    @pl.loop(0, TILES)
    def _(t):
        for x in range(CHUNKS):
            lanes = pl.ds(x * LANES, LANES)
            mat = matrix(lambda c: tile_grad[t, c, pl.ds(x, 1), :], relax[t, pl.ds(x, 1), :])
            state = [base[t, c, :, lanes] for c in range(3)]
            noise = [base_noise[1, t, c, :, lanes] for c in range(3)]
            state = advance(mat, state, noise)
            for c in range(3):
                base[t, c, :, lanes] = state[c]
            for m, total in enumerate(products(state)):
                own_moment[t, m, pl.ds(x, 1), :] = row_sum(total)

    for copy in moment_copies:
        copy.wait_recv()
    for t in range(TILES):
        count = jnp.full((CHUNKS, LANES), counts[t], jnp.int32).astype(F32)
        second = [
            (own_moment[t, m] + jnp.where(found[t] == 1, moment_recv[slot_of[t], m], 0.0)) / count
            for m in range(6)
        ]
        trace = second[0] + second[1] + second[2]
        stretch = 1.0 / (1.0 - trace / max_extension)
        for m in range(6):
            value = (stretch * second[m] - (1.0 if m < 3 else 0.0)) / weissenberg
            for x in range(CHUNKS):
                stress[m, pl.ds(t, 1), pl.ds(x * LANES, LANES)] = value[x : x + 1]

    for copies in (halo_copies, first_sums, grad_copies, second_sums, moment_copies):
        for copy in copies:
            copy.wait_send()


def solution(mesh):
    n_gx, n_gy = mesh.shape["gx"], mesh.shape["gy"]

    def per_device(
        velocity,
        wall_cells,
        tile_counts,
        helper_tile,
        base_fields,
        extra_fields,
        base_noise,
        extra_noise,
    ):
        hbm_spec = pl.BlockSpec(memory_space=pltpu.HBM)
        vmem_spec = pl.BlockSpec(memory_space=pltpu.VMEM)
        smem_spec = pl.BlockSpec(memory_space=pltpu.SMEM)
        dma = pltpu.SemaphoreType.DMA

        def hold(array):
            return pltpu.with_memory_space_constraint(array, pltpu.HBM)

        base_out, extra_out, stress_out = pl.pallas_call(
            functools.partial(kernel, n_gx, n_gy),
            out_shape=(
                jax.ShapeDtypeStruct((TILES, 3, BASE, CELLS), F32),
                jax.ShapeDtypeStruct((3, EXTRA, CELLS), F32),
                jax.ShapeDtypeStruct((6, TILES, CELLS), F32),
            ),
            in_specs=[smem_spec, smem_spec] + [hbm_spec] * 6,
            out_specs=(vmem_spec, vmem_spec, vmem_spec),
            scratch_shapes=[
                pltpu.VMEM((3, 8, 8, LANES), F32),
                pltpu.VMEM((8, 8, LANES), jnp.int32),
                pltpu.VMEM((STEPS, TILES, 3, BASE, CELLS), jnp.bfloat16),
                pltpu.VMEM((STEPS, 3, EXTRA, CELLS), jnp.bfloat16),
                pltpu.VMEM((2, 3, 8, LANES), F32),
                pltpu.VMEM((2, 3, 8, LANES), F32),
                pltpu.VMEM((2, 3, 8, LANES), F32),
                pltpu.VMEM((TILES, 9, CHUNKS, LANES), F32),
                pltpu.VMEM((9, CHUNKS, LANES), F32),
                pltpu.VMEM((n_gy, 9, CHUNKS, LANES), F32),
                pltpu.VMEM((n_gy, 9, CHUNKS, LANES), F32),
                pltpu.VMEM((TILES, CHUNKS, LANES), F32),
                pltpu.VMEM((CHUNKS, LANES), F32),
                pltpu.VMEM((STEPS, n_gy, 2, CHUNKS, LANES), F32),
                pltpu.VMEM((n_gy, 2, CHUNKS, LANES), F32),
                pltpu.VMEM((n_gy, 2, CHUNKS, LANES), F32),
                pltpu.VMEM((TILES, CHUNKS, LANES), F32),
                pltpu.VMEM((CHUNKS, LANES), F32),
                pltpu.VMEM((TILES, 6, CHUNKS, LANES), F32),
                pltpu.VMEM((n_gy, 6, CHUNKS, LANES), F32),
                dma((7,)),
                dma((TILES,)),
                dma((4,)),
                dma((4,)),
                dma((n_gy,)),
                dma((n_gy,)),
                dma((STEPS, n_gy)),
                dma((STEPS, n_gy)),
                dma((n_gy,)),
                dma((n_gy,)),
            ],
            compiler_params=pltpu.CompilerParams(
                collective_id=0, has_side_effects=True, vmem_limit_bytes=40 << 20
            ),
        )(
            hold(tile_counts.reshape(TILES)),
            hold(helper_tile.reshape(n_gy)),
            hold(velocity),
            hold(wall_cells),
            hold(base_fields.reshape(TILES, 3, BASE, CELLS)),
            hold(extra_fields.reshape(3, EXTRA, CELLS)),
            hold(base_noise.reshape(TILES, STEPS, 3, BASE, CELLS)),
            hold(extra_noise.reshape(STEPS, 3, EXTRA, CELLS)),
        )
        return base_out[None, None], extra_out[None, None], stress_out.transpose(1, 0, 2)[None, None]

    in_specs = (
        P(None, "gx", "gy", None),
        P("gx", "gy", None),
        P("gx", "gy", None),
        P("gx", None),
        P("gx", "gy", None, None, None, None),
        P("gx", "gy", None, None, None),
        P("gx", "gy", None, None, None, None, None),
        P("gx", "gy", None, None, None, None),
    )
    out_specs = (
        P("gx", "gy", None, None, None, None),
        P("gx", "gy", None, None, None),
        P("gx", "gy", None, None, None),
    )
    return jax.shard_map(
        per_device, mesh=mesh, in_specs=in_specs, out_specs=out_specs, check_vma=False
    )
```

time: 231 us -> 41.2 us (0.18)
  blocking collectives: 119 us -> 0 us
  other arithmetic: 47.3 us -> 0 us
  Pallas kernels: 0 us -> 36.6 us
  local copies, waits for them, and re-layouts: 37.2 us -> 3.88 us
  starting transfers between devices: 15.7 us -> 0 us
  waiting for transfers between devices: 8.16 us -> 0 us
    all_gather x5 -> x0, blocking collectives: 119 us -> none  [the longest x3 71.6 us: partner_totals(): lax.all_gather(extra_rows[None], 'gy', axis=0, tiled=True)]
    pallas_call x0 -> x1, Pallas kernels: none -> 36.6 us  [per_device(): pl.pallas_call(functools.partial(kernel, n_gx, n_gy), out_shape=(jax.Shap...]
    add x13 -> x0, other arithmetic: 21.4 us -> none  [the longest x11 21.4 us: advance(): current + time_step * (drift - relax * current)]
    reduce_sum x16 -> x0, other arithmetic: 12 us -> none  [the longest x2 2.73 us: per_device(): base_square = jnp.sum(base_state * base_state, axis=(1, 2))]
    ppermute x4 -> x0, starting transfers between devices: 11.4 us -> none  [the longest x2 6.46 us: extended(): before = lax.ppermute(last, axis, up)]
    another operation x11 -> x0, local copies, waits for them, and re-layouts: 8.37 us -> none  [the longest x9 6.28 us: moments(): jnp.stack([jnp.sum(state[..., first_axis, :, :] * state[..., second_axis,...]
    all_to_all x1 -> x0, waiting for transfers between devices: 8.15 us -> none  [per_device(): lax.all_to_all(outgoing, 'gy', split_axis=0, concat_axis=0, tiled=True)]
    unnamed x122 -> x3, local copies, waits for them, and re-layouts: 10.5 us -> 3.88 us
  transfers between devices with their start and end apart: 5 -> 0, of which waited for: 1 -> 0; matrix products, arithmetic and copies ran while one was open for 8% -> 0% of each run, Pallas kernels for 0% -> 0%
where the time goes in v1:
time: 41.2 us; the launch traced here: 41.1 us
  Pallas kernels  36.6 us (89%)
  local copies, waits for them, and re-layouts  3.88 us (9%)
  between operations  0.64 us (2%)
    pallas_call x1, Pallas kernels, per_device(): pl.pallas_call(functools.partial(kernel, n_gx, n_gy), out_shape=(jax.Shap...  36.6 us
    unnamed x3, local copies, waits for them, and re-layouts  3.88 us

profile of v1, /device:TPU:32, one launch (start us, length us, event | category | flops | bytes accessed | tf_op | source)
XLA Modules:
  0.0 41.1 jit_solution(12851632667492380943)
XLA Ops:
  0.6 36.6 %shard_map.103 = (f32[8,3,32,1024]{3,2,1,0:T(8,128)S(1)}, f32[3,224,1024]{2,1,0:T(8,128)S(1)}, f32[6,8,1024]{2,1,0:T(8,128)S(1)}) custom-call(s32[8]{0:T(128)} %bitcast.18, s32[16]{0:T(128)} %bitcast.19, f32[3,8,8,128]{3,2,1,0:T(8,128)} %vel_hbm.1, s32[8,8,128]{2,1,0:T(8,128)} %wall_hbm.1, f32[8,3,32,1024]{3,2,1,0:T(8,128)} %bitcast.14, ...), custom_call_target="tpu_custom_call" | custom-call | tf_op jit(solution)/shard_map/pallas_call | solution.py:436
  37.2 1.7 %copy.14 = f32[1,1,8,3,32,1024]{5,4,3,2,1,0:T(8,128)} copy(f32[1,1,8,3,32,1024]{5,4,3,2,1,0:T(8,128)S(1)} %bitcast.11) | data formatting | bytes 6291456
  38.9 1.5 %copy.15 = f32[1,1,3,224,1024]{4,3,2,1,0:T(8,128)} copy(f32[1,1,3,224,1024]{4,3,2,1,0:T(8,128)S(1)} %bitcast.12) | data formatting | bytes 5505024
  40.4 0.7 %copy.16 = f32[1,1,8,6,1024]{4,2,3,1,0:T(8,128)} copy(f32[1,1,8,6,1024]{4,2,3,1,0:T(8,128)S(1)} %bitcast.13) | data formatting | bytes 393216

commit v2 on v1

v2 whole, which is shorter than its diff:
```python
import functools

import jax
import jax.numpy as jnp
from jax import lax
from jax.experimental import pallas as pl
from jax.experimental.pallas import tpu as pltpu
from jax.sharding import PartitionSpec as P

MESH = pl.DeviceIdType.MESH
F32 = jnp.float32

STEPS = 2
TILES = 8
CELLS = 1024
LANES = 128
CHUNKS = CELLS // LANES
BASE = 32
EXTRA = 224
GROUP = 32
PARTS = 2
ROWS = CHUNKS // PARTS

time_step = 0.05
weissenberg = 0.25
max_extension = 50.0
noise_scale = (time_step / weissenberg) ** 0.5
relax_scale = time_step * (0.5 / weissenberg)
component_pairs = ((0, 0), (1, 1), (2, 2), (0, 1), (0, 2), (1, 2))


def wide(row):
    return jnp.broadcast_to(row, (GROUP, LANES))


def matrix(grad_row, keep_row):
    keep = wide(keep_row)
    rows = []
    for a in range(3):
        row = [wide(grad_row(3 * a + b)) for b in range(3)]
        row[a] = row[a] + keep
        rows.append(row)
    return rows


def advance(mat, state, noise):
    return [
        mat[a][0] * state[0]
        + mat[a][1] * state[1]
        + mat[a][2] * state[2]
        + noise_scale * noise[a].astype(F32)
        for a in range(3)
    ]


def fold(block):
    out = block[:8]
    for k in range(1, block.shape[0] // 8):
        out = out + block[8 * k : 8 * k + 8]
    return out


def inner(left, right):
    return fold(left[0] * right[0] + left[1] * right[1] + left[2] * right[2])


def products(state):
    return [fold(state[a] * state[b]) for a, b in component_pairs]


def row_sum(block):
    return jnp.sum(block, axis=0, keepdims=True)


def relaxation(total, count):
    return relax_scale * (1.0 / (1.0 - total / count / max_extension))


def part_of(value, p):
    return value[p * ROWS : (p + 1) * ROWS]


def helper_slots(helper, gy, n_gy, t):
    slot, hit = jnp.int32(0), jnp.int32(0)
    for h in range(n_gy):
        match = helper[h] == gy * TILES + t
        slot = jnp.where(match, lax.rem(gy - h + n_gy, n_gy), slot)
        hit = jnp.where(match, 1, hit)
    return slot, hit


def exchange_kernel(
    n_gx,
    n_gy,
    counts,
    helper,
    vel_hbm,
    wall_hbm,
    base_hbm,
    extra_hbm,
    base_noise_hbm,
    extra_noise_hbm,
    base,
    extra,
    late_noise,
    tile_grad,
    own_total,
    moment_recv,
    vel,
    wall,
    drifted,
    base_noise,
    extra_noise,
    y_edge,
    x_halo,
    y_halo,
    own_sums,
    extra_sum,
    extra_recv,
    own_send,
    own_recv,
    helper_relax,
    helper_total,
    row_total,
    relax,
    *rest,
):
    grad_send, grad_recv = rest[:PARTS], rest[PARTS : 2 * PARTS]
    (
        in_sem,
        tile_sem,
        halo_send_sem,
        halo_recv_sem,
        extra_send_sem,
        extra_recv_sem,
        own_send_sem,
        own_recv_sem,
        grad_send_sem,
        grad_recv_sem,
        moment_send_sem,
        moment_recv_sem,
    ) = rest[2 * PARTS :]
    gx = lax.axis_index("gx")
    gy = lax.axis_index("gy")
    up_x, down_x = lax.rem(gx + 1, n_gx), lax.rem(gx + n_gx - 1, n_gx)
    up_y, down_y = lax.rem(gy + 1, n_gy), lax.rem(gy + n_gy - 1, n_gy)

    vel_copy = pltpu.make_async_copy(vel_hbm, vel, in_sem.at[0])
    wall_copy = pltpu.make_async_copy(wall_hbm, wall, in_sem.at[1])
    extra_copy = pltpu.make_async_copy(extra_hbm, extra, in_sem.at[2])
    base_copies = [
        pltpu.make_async_copy(base_hbm.at[t], base.at[t], tile_sem.at[t]) for t in range(TILES)
    ]
    base_noise_copies = [
        pltpu.make_async_copy(base_noise_hbm.at[:, 0], base_noise, in_sem.at[3]),
        pltpu.make_async_copy(base_noise_hbm.at[:, 1], late_noise, in_sem.at[4]),
    ]
    extra_noise_copies = [
        pltpu.make_async_copy(extra_noise_hbm.at[s], extra_noise.at[s], in_sem.at[5 + s])
        for s in range(STEPS)
    ]
    vel_copy.start()
    wall_copy.start()
    extra_copy.start()
    for copy in base_copies:
        copy.start()
    for s in range(STEPS):
        base_noise_copies[s].start()
        extra_noise_copies[s].start()

    barrier = pltpu.get_barrier_semaphore()
    for k in range(1, n_gy):
        peer = lax.rem(gy + k, n_gy)
        pl.semaphore_signal(barrier, inc=1, device_id=(gx, peer), device_id_type=MESH)
    for peer in (up_x, down_x):
        pl.semaphore_signal(barrier, inc=1, device_id=(peer, gy), device_id_type=MESH)

    my_slot = lax.rem(gy - helper[gy] // TILES + n_gy, n_gy)
    slots = [helper_slots(helper, gy, n_gy, t) for t in range(TILES)]

    vel_copy.wait()
    for c in range(3):
        y_edge[0, c] = vel[c, :, 7, :]
        y_edge[1, c] = vel[c, :, 0, :]
    pl.semaphore_wait(barrier, n_gy + 1)

    halo_copies = [
        pltpu.make_async_remote_copy(
            src_ref=src,
            dst_ref=dst,
            send_sem=halo_send_sem.at[i],
            recv_sem=halo_recv_sem.at[i],
            device_id=device,
            device_id_type=MESH,
        )
        for i, (src, dst, device) in enumerate(
            (
                (vel.at[:, 7], x_halo.at[0], (up_x, gy)),
                (vel.at[:, 0], x_halo.at[1], (down_x, gy)),
                (y_edge.at[0], y_halo.at[0], (gx, up_y)),
                (y_edge.at[1], y_halo.at[1], (gx, down_y)),
            )
        )
    ]
    for copy in halo_copies:
        copy.start()

    def send_all(src_of, dst_of, send_sem, recv_sem):
        copies = [
            pltpu.make_async_remote_copy(
                src_ref=src_of(k),
                dst_ref=dst_of(k),
                send_sem=send_sem(k),
                recv_sem=recv_sem(k),
                device_id=(gx, lax.rem(gy + k, n_gy)),
                device_id_type=MESH,
            )
            for k in range(1, n_gy)
        ]
        for copy in copies:
            copy.start()
        return copies

    extra_copy.wait()

    @pl.loop(0, CHUNKS)
    def _(x):
        lanes = pl.ds(pl.multiple_of(x * LANES, LANES), LANES)
        total = jnp.zeros((8, LANES), F32)
        for f in range(EXTRA // GROUP):
            state = [extra[c, pl.ds(f * GROUP, GROUP), lanes] for c in range(3)]
            total = total + inner(state, state)
        extra_sum[pl.ds(x, 1), :] = row_sum(total)

    wall_copy.wait()
    for copy in halo_copies:
        copy.wait_recv()
    sub = lax.broadcasted_iota(jnp.int32, (8, LANES), 0)
    lane = lax.broadcasted_iota(jnp.int32, (8, LANES), 1)
    block = lane // 16
    fluid = [
        jnp.where(wall[:, y, :] == 0, 0.5 * time_step, 0.0).astype(F32) for y in range(8)
    ]
    for a in range(3):
        here = [vel[a, :, y, :] for y in range(8)]
        low_y = jnp.where(gy > 0, y_halo[0, a], 0.0)
        high_y = jnp.where(gy < n_gy - 1, y_halo[1, a], 0.0)
        padded = [low_y] + here + [high_y]
        low_x = jnp.where(gx > 0, x_halo[0, a], 0.0)
        high_x = jnp.where(gx < n_gx - 1, x_halo[1, a], 0.0)
        columns = [[], [], []]
        for y in range(8):
            v = here[y]
            low = jnp.broadcast_to(low_x[y : y + 1], (8, LANES))
            high = jnp.broadcast_to(high_x[y : y + 1], (8, LANES))
            before = jnp.where(sub == 0, low, pltpu.roll(v, 1, 0))
            after = jnp.where(sub == 7, high, pltpu.roll(v, 7, 0))
            columns[0].append((after - before) * fluid[y])
            columns[1].append((padded[y + 2] - padded[y]) * fluid[y])
            before = jnp.where(lane == 0, 0.0, pltpu.roll(v, 1, 1))
            after = jnp.where(lane == LANES - 1, 0.0, pltpu.roll(v, LANES - 1, 1))
            columns[2].append((after - before) * fluid[y])
        for b in range(3):
            regs = columns[b]
            for bit in (1, 2, 4):
                upper = (block & bit) != 0
                new = list(regs)
                for i in range(8):
                    if i & bit:
                        continue
                    j = i | bit
                    new[i] = jnp.where(upper, pltpu.roll(regs[j], 16 * bit, 1), regs[i])
                    new[j] = jnp.where(upper, regs[j], pltpu.roll(regs[i], LANES - 16 * bit, 1))
                regs = new
            for t in range(TILES):
                for p in range(PARTS):
                    tile_grad[t, p, 3 * a + b] = part_of(regs[t], p)

    extra_copies = send_all(
        lambda k: extra_sum,
        lambda k: extra_recv.at[k],
        lambda k: extra_send_sem.at[k],
        lambda k: extra_recv_sem.at[k],
    )
    extra_recv[0] = extra_sum[...]

    grad_copies = []
    for p in range(PARTS):

        @pl.loop(0, n_gy)
        def _(k):
            tile = lax.rem(helper[lax.rem(gy + k, n_gy)], TILES)
            grad_send[p][k] = tile_grad[tile, p]

        grad_copies.append(
            send_all(
                lambda k: grad_send[p].at[k],
                lambda k: grad_recv[p].at[k],
                lambda k: grad_send_sem.at[p, k],
                lambda k: grad_recv_sem.at[p, k],
            )
        )
        grad_recv[p][0] = grad_send[p][0]

    for copy in base_copies:
        copy.wait()
    base_noise_copies[0].wait()

    @pl.loop(0, TILES)
    def _(t):
        for x in range(CHUNKS):
            lanes = pl.ds(x * LANES, LANES)
            p, r = divmod(x, ROWS)
            mat = matrix(lambda c: tile_grad[t, p, c, pl.ds(r, 1), :], jnp.ones((1, LANES), F32))
            state = [base[t, c, :, lanes] for c in range(3)]
            noise = [base_noise[t, c, :, lanes] for c in range(3)]
            moved = advance(mat, state, noise)
            for c in range(3):
                drifted[t, c, :, lanes] = moved[c]
            own_sums[t, 0, pl.ds(x, 1), :] = row_sum(inner(state, state))
            own_sums[t, 1, pl.ds(x, 1), :] = row_sum(inner(state, moved))
            own_sums[t, 2, pl.ds(x, 1), :] = row_sum(inner(moved, moved))

    @pl.loop(0, n_gy)
    def _(k):
        tile = lax.rem(helper[lax.rem(gy + k, n_gy)], TILES)
        own_send[k] = own_sums[tile]

    own_copies = send_all(
        lambda k: own_send.at[k],
        lambda k: own_recv.at[k],
        lambda k: own_send_sem.at[k],
        lambda k: own_recv_sem.at[k],
    )
    own_recv[0] = own_send[0]

    for copy in extra_copies:
        copy.wait_recv()
    for t in range(TILES):
        slot, hit = slots[t]
        count = jnp.full((CHUNKS, LANES), counts[t], jnp.int32).astype(F32)
        total = own_sums[t, 0] + jnp.where(hit == 1, extra_recv[slot], 0.0)
        rate = relaxation(total, count)
        relax[t] = rate
        own = own_sums[t, 2] - rate * (2.0 * own_sums[t, 1] - rate * own_sums[t, 0])
        for p in range(PARTS):
            own_total[t, p] = part_of(own, p)

    @pl.loop(0, TILES)
    def _(t):
        for x in range(CHUNKS):
            lanes = pl.ds(x * LANES, LANES)
            rate = wide(relax[t, pl.ds(x, 1), :])
            for c in range(3):
                base[t, c, :, lanes] = drifted[t, c, :, lanes] - rate * base[t, c, :, lanes]

    for copy in own_copies:
        copy.wait_recv()
    sums = [own_recv[my_slot, m] for m in range(3)]
    rate = relaxation(sums[0] + extra_sum[...], 256.0)
    helper_relax[...] = rate
    helper_total[...] = sums[2] - rate * (2.0 * sums[1] - rate * sums[0])

    for copy in extra_noise_copies:
        copy.wait()
    moment_copies = []
    for p in range(PARTS):
        for copy in grad_copies[p]:
            copy.wait_recv()

        @pl.loop(0, ROWS)
        def _(r):
            x = p * ROWS + r
            lanes = pl.ds(pl.multiple_of(x * LANES, LANES), LANES)
            mat = matrix(
                lambda c: grad_recv[p][my_slot, c, pl.ds(r, 1), :],
                1.0 - helper_relax[pl.ds(x, 1), :],
            )
            total = jnp.zeros((8, LANES), F32)
            for f in range(EXTRA // GROUP):
                fields = pl.ds(f * GROUP, GROUP)
                state = [extra[c, fields, lanes] for c in range(3)]
                noise = [extra_noise[0, c, fields, lanes] for c in range(3)]
                state = advance(mat, state, noise)
                for c in range(3):
                    extra[c, fields, lanes] = state[c]
                total = total + inner(state, state)
            row_total[pl.ds(x, 1), :] = row_sum(total)

        here = row_total[pl.ds(p * ROWS, ROWS), :]
        moment_recv[0, p, 6] = here
        helper_relax[pl.ds(p * ROWS, ROWS), :] = relaxation(
            here + helper_total[pl.ds(p * ROWS, ROWS), :], 256.0
        )

        @pl.loop(0, ROWS)
        def _(r):
            x = p * ROWS + r
            lanes = pl.ds(pl.multiple_of(x * LANES, LANES), LANES)
            mat = matrix(
                lambda c: grad_recv[p][my_slot, c, pl.ds(r, 1), :],
                1.0 - helper_relax[pl.ds(x, 1), :],
            )
            totals = [jnp.zeros((8, LANES), F32) for _ in range(6)]
            for f in range(EXTRA // GROUP):
                fields = pl.ds(f * GROUP, GROUP)
                state = [extra[c, fields, lanes] for c in range(3)]
                noise = [extra_noise[1, c, fields, lanes] for c in range(3)]
                state = advance(mat, state, noise)
                for c in range(3):
                    extra[c, fields, lanes] = state[c]
                totals = [u + v for u, v in zip(totals, products(state))]
            for m in range(6):
                moment_recv[0, p, m, pl.ds(r, 1), :] = row_sum(totals[m])

        moment_copies.append(
            send_all(
                lambda k: moment_recv.at[0, p],
                lambda k: moment_recv.at[k, p],
                lambda k: moment_send_sem.at[p, k],
                lambda k: moment_recv_sem.at[p, k],
            )
        )

    base_noise_copies[1].wait()
    for copies in (halo_copies, extra_copies, own_copies, *grad_copies):
        for copy in copies:
            copy.wait_send()
    for copies in moment_copies:
        for copy in copies:
            copy.wait_recv()
            copy.wait_send()


def finish_kernel(
    n_gy,
    counts,
    helper,
    start,
    extra,
    noise,
    tile_grad,
    own_total,
    moment_recv,
    base_out,
    extra_out,
    stress_out,
    base,
    stress,
    staged,
    relax,
    moment,
    tile_sem,
    out_sem,
):
    gy = lax.axis_index("gy")
    extra_copy = pltpu.make_async_copy(extra, extra_out, out_sem.at[0])
    extra_copy.start()

    @pl.loop(0, TILES)
    def _(t):
        slot, hit = helper_slots(helper, gy, n_gy, t)
        heavy = hit == 1
        count = jnp.full((ROWS, LANES), counts[t], jnp.int32).astype(F32)
        for p in range(PARTS):
            total = own_total[t, p] + jnp.where(heavy, moment_recv[slot, p, 6], 0.0)
            relax[p] = relaxation(total, count)
        for x in range(CHUNKS):
            lanes = pl.ds(x * LANES, LANES)
            p, r = divmod(x, ROWS)
            mat = matrix(
                lambda c: tile_grad[t, p, c, pl.ds(r, 1), :], 1.0 - relax[p, pl.ds(r, 1), :]
            )
            state = [start[t, c, :, lanes] for c in range(3)]
            state = advance(mat, state, [noise[t, c, :, lanes] for c in range(3)])
            for c in range(3):
                base[t, c, :, lanes] = state[c]
            for m, total in enumerate(products(state)):
                moment[p, m, pl.ds(r, 1), :] = row_sum(total)
        pltpu.make_async_copy(base.at[t], base_out.at[t], tile_sem.at[t]).start()
        for p in range(PARTS):
            second = [
                (moment[p, m] + jnp.where(heavy, moment_recv[slot, p, m], 0.0)) / count
                for m in range(6)
            ]
            trace = second[0] + second[1] + second[2]
            stretch = 1.0 / (1.0 - trace / max_extension)
            for m in range(6):
                value = (stretch * second[m] - (1.0 if m < 3 else 0.0)) / weissenberg
                for r in range(ROWS):
                    staged[m, p * ROWS + r, pl.ds(t, 1), :] = value[r : r + 1]

    for m in range(6):
        for x in range(CHUNKS):
            stress[m, :, pl.ds(x * LANES, LANES)] = staged[m, x]
    stress_copy = pltpu.make_async_copy(stress, stress_out, out_sem.at[1])
    stress_copy.start()
    for t in range(TILES):
        pltpu.make_async_copy(base.at[t], base_out.at[t], tile_sem.at[t]).wait()
    extra_copy.wait()
    stress_copy.wait()


def hold(array):
    return pltpu.with_memory_space_constraint(array, pltpu.HBM)


def solution(mesh):
    n_gx, n_gy = mesh.shape["gx"], mesh.shape["gy"]

    def per_device(
        velocity,
        wall_cells,
        tile_counts,
        helper_tile,
        base_fields,
        extra_fields,
        base_noise,
        extra_noise,
    ):
        hbm = pl.BlockSpec(memory_space=pltpu.HBM)
        vmem = pl.BlockSpec(memory_space=pltpu.VMEM)
        smem = pl.BlockSpec(memory_space=pltpu.SMEM)
        dma = pltpu.SemaphoreType.DMA
        counts = hold(tile_counts.reshape(TILES))
        helper = hold(helper_tile.reshape(n_gy))
        grad_buffer = pltpu.VMEM((n_gy, 9, ROWS, LANES), F32)
        passed = pl.pallas_call(
            functools.partial(exchange_kernel, n_gx, n_gy),
            out_shape=(
                jax.ShapeDtypeStruct((TILES, 3, BASE, CELLS), F32),
                jax.ShapeDtypeStruct((3, EXTRA, CELLS), F32),
                jax.ShapeDtypeStruct((TILES, 3, BASE, CELLS), jnp.bfloat16),
                jax.ShapeDtypeStruct((TILES, PARTS, 9, ROWS, LANES), F32),
                jax.ShapeDtypeStruct((TILES, PARTS, ROWS, LANES), F32),
                jax.ShapeDtypeStruct((n_gy, PARTS, 7, ROWS, LANES), F32),
            ),
            in_specs=[smem] * 2 + [hbm] * 6,
            out_specs=(vmem,) * 6,
            scratch_shapes=[
                pltpu.VMEM((3, 8, 8, LANES), F32),
                pltpu.VMEM((8, 8, LANES), jnp.int32),
                pltpu.VMEM((TILES, 3, BASE, CELLS), F32),
                pltpu.VMEM((TILES, 3, BASE, CELLS), jnp.bfloat16),
                pltpu.VMEM((STEPS, 3, EXTRA, CELLS), jnp.bfloat16),
                pltpu.VMEM((2, 3, 8, LANES), F32),
                pltpu.VMEM((2, 3, 8, LANES), F32),
                pltpu.VMEM((2, 3, 8, LANES), F32),
                pltpu.VMEM((TILES, 3, CHUNKS, LANES), F32),
                pltpu.VMEM((CHUNKS, LANES), F32),
                pltpu.VMEM((n_gy, CHUNKS, LANES), F32),
                pltpu.VMEM((n_gy, 3, CHUNKS, LANES), F32),
                pltpu.VMEM((n_gy, 3, CHUNKS, LANES), F32),
                pltpu.VMEM((CHUNKS, LANES), F32),
                pltpu.VMEM((CHUNKS, LANES), F32),
                pltpu.VMEM((CHUNKS, LANES), F32),
                pltpu.VMEM((TILES, CHUNKS, LANES), F32),
                *[grad_buffer] * (2 * PARTS),
                dma((7,)),
                dma((TILES,)),
                dma((4,)),
                dma((4,)),
                dma((n_gy,)),
                dma((n_gy,)),
                dma((n_gy,)),
                dma((n_gy,)),
                dma((PARTS, n_gy)),
                dma((PARTS, n_gy)),
                dma((PARTS, n_gy)),
                dma((PARTS, n_gy)),
            ],
            compiler_params=pltpu.CompilerParams(
                collective_id=0, has_side_effects=True, vmem_limit_bytes=40 << 20
            ),
        )(
            counts,
            helper,
            hold(velocity),
            hold(wall_cells),
            hold(base_fields.reshape(TILES, 3, BASE, CELLS)),
            hold(extra_fields.reshape(3, EXTRA, CELLS)),
            hold(base_noise.reshape(TILES, STEPS, 3, BASE, CELLS)),
            hold(extra_noise.reshape(STEPS, 3, EXTRA, CELLS)),
        )
        base_out, extra_out, stress_out = pl.pallas_call(
            functools.partial(finish_kernel, n_gy),
            out_shape=(
                jax.ShapeDtypeStruct((TILES, 3, BASE, CELLS), F32),
                jax.ShapeDtypeStruct((3, EXTRA, CELLS), F32),
                jax.ShapeDtypeStruct((6, TILES, CELLS), F32),
            ),
            in_specs=[smem] * 2 + [vmem] * 6,
            out_specs=(hbm,) * 3,
            scratch_shapes=[
                pltpu.VMEM((TILES, 3, BASE, CELLS), F32),
                pltpu.VMEM((6, TILES, CELLS), F32),
                pltpu.VMEM((6, CHUNKS, TILES, LANES), F32),
                pltpu.VMEM((PARTS, ROWS, LANES), F32),
                pltpu.VMEM((PARTS, 6, ROWS, LANES), F32),
                dma((TILES,)),
                dma((2,)),
            ],
            compiler_params=pltpu.CompilerParams(vmem_limit_bytes=40 << 20),
        )(counts, helper, *passed)
        return base_out[None, None], extra_out[None, None], stress_out.transpose(1, 0, 2)[None, None]

    in_specs = (
        P(None, "gx", "gy", None),
        P("gx", "gy", None),
        P("gx", "gy", None),
        P("gx", None),
        P("gx", "gy", None, None, None, None),
        P("gx", "gy", None, None, None),
        P("gx", "gy", None, None, None, None, None),
        P("gx", "gy", None, None, None, None),
    )
    out_specs = (
        P("gx", "gy", None, None, None, None),
        P("gx", "gy", None, None, None),
        P("gx", "gy", None, None, None),
    )
    return jax.shard_map(
        per_device, mesh=mesh, in_specs=in_specs, out_specs=out_specs, check_vma=False
    )
```

time: 41.2 us -> 38.7 us (0.939)
  local copies, waits for them, and re-layouts: 3.88 us -> 0 us
  Pallas kernels: 36.6 us -> 38 us
    unnamed x3 -> x0, local copies, waits for them, and re-layouts: 3.88 us -> none
    pallas_call x1 -> x2, Pallas kernels: 36.6 us -> 38 us  [the longest x1 34.2 us: per_device(): pl.pallas_call(functools.partial(exchange_kernel, n_gx, n_gy), out_shape=...]
where the time goes in v2:
time: 38.7 us; the launch traced here: 38.6 us
  Pallas kernels  38 us (98%)
  between operations  0.64 us (2%)
    pallas_call x1, Pallas kernels, per_device(): pl.pallas_call(functools.partial(exchange_kernel, n_gx, n_gy), out_shape=...  34.2 us
    pallas_call x1, Pallas kernels, per_device(): pl.pallas_call(functools.partial(finish_kernel, n_gy), out_shape=(jax.Sha...  3.77 us

profile of v2, /device:TPU:32, one launch (start us, length us, event | category | flops | bytes accessed | tf_op | source)
XLA Modules:
  0.0 38.6 jit_solution(10249348432751426382)
XLA Ops:
  0.6 34.2 %shard_map.103 = (f32[8,3,32,1024]{3,2,1,0:T(8,128)S(1)}, f32[3,224,1024]{2,1,0:T(8,128)S(1)}, bf16[8,3,32,1024]{3,2,1,0:T(8,128)(2,1)S(1)}, f32[8,2,9,4,128]{4,...) custom-call(s32[8]{0:T(128)} %bitcast.15, s32[16]{0:T(128)} %bitcast.17, ...), custom_call_target="tpu_custom_call" | custom-call | tf_op jit(solution)/shard_map/pallas_call | solution.py:528
  34.8 3.8 %shard_map.104 = (f32[8,3,32,1024]{3,2,1,0:T(8,128)}, f32[3,224,1024]{2,1,0:T(8,128)}, f32[6,8,1024]{2,1,0:T(8,128)}) custom-call(s32[8]{0:T(128)} %bitcast.16, s32[16]{0:T(128)} %bitcast.18, f32[8,3,32,1024]{3,2,1,0:T(8,128)S(1)} %get-tuple-element.12.start, f32[3,224,1024]{2,1,0:T(8,128)S(1)} %get-tuple-element.13.extra, ...), custom_call_target="tpu_custom_call" | custom-call | tf_op jit(solution)/shard_map/pallas_call | solution.py:585

commit v3 on v2

v3 whole, which is shorter than its diff:
```python
import functools

import jax
import jax.numpy as jnp
from jax import lax
from jax.experimental import pallas as pl
from jax.experimental.pallas import tpu as pltpu
from jax.sharding import PartitionSpec as P

MESH = pl.DeviceIdType.MESH
F32 = jnp.float32

STEPS = 2
TILES = 8
CELLS = 1024
LANES = 128
CHUNKS = CELLS // LANES
BASE = 32
EXTRA = 224
GROUP = 32
PARTS = 2
ROWS = CHUNKS // PARTS

time_step = 0.05
weissenberg = 0.25
max_extension = 50.0
noise_scale = (time_step / weissenberg) ** 0.5
relax_scale = time_step * (0.5 / weissenberg)
component_pairs = ((0, 0), (1, 1), (2, 2), (0, 1), (0, 2), (1, 2))


def wide(row):
    return jnp.broadcast_to(row, (GROUP, LANES))


def matrix(grad_row, keep_row):
    keep = wide(keep_row)
    rows = []
    for a in range(3):
        row = [wide(grad_row(3 * a + b)) for b in range(3)]
        row[a] = row[a] + keep
        rows.append(row)
    return rows


def advance(mat, state, noise):
    return [
        mat[a][0] * state[0]
        + mat[a][1] * state[1]
        + mat[a][2] * state[2]
        + noise_scale * noise[a].astype(F32)
        for a in range(3)
    ]


def fold(block):
    out = block[:8]
    for k in range(1, block.shape[0] // 8):
        out = out + block[8 * k : 8 * k + 8]
    return out


def inner(left, right):
    return fold(left[0] * right[0] + left[1] * right[1] + left[2] * right[2])


def products(state):
    return [fold(state[a] * state[b]) for a, b in component_pairs]


def row_sum(block):
    return jnp.sum(block, axis=0, keepdims=True)


def relaxation(total, count):
    return relax_scale * (1.0 / (1.0 - total / count / max_extension))


def helper_slots(helper, gy, n_gy, t):
    slot, hit = jnp.int32(0), jnp.int32(0)
    for h in range(n_gy):
        match = helper[h] == gy * TILES + t
        slot = jnp.where(match, lax.rem(gy - h + n_gy, n_gy), slot)
        hit = jnp.where(match, 1, hit)
    return slot, hit


def swap_blocks(regs, block):
    for bit in (1, 2, 4):
        upper = (block & bit) != 0
        new = list(regs)
        for i in range(8):
            if i & bit:
                continue
            j = i | bit
            new[i] = jnp.where(upper, pltpu.roll(regs[j], 16 * bit, 1), regs[i])
            new[j] = jnp.where(upper, regs[j], pltpu.roll(regs[i], LANES - 16 * bit, 1))
        regs = new
    return regs


def gradient(velocity, z_edge, fluid, y_edge, x_edge, sub, lane):
    deep = lane % 16

    def turn(value, shift):
        shift = shift % LANES
        return pltpu.roll(value, shift, 1) if shift else value

    grads = []
    for a in range(3):
        v = velocity[a]
        low = jnp.broadcast_to(x_edge[a : a + 1], (8, LANES))
        high = jnp.broadcast_to(x_edge[3 + a : 4 + a], (8, LANES))
        before = jnp.where(sub == 0, low, pltpu.roll(v, 1, 0))
        after = jnp.where(sub == 7, high, pltpu.roll(v, 7, 0))
        grads.append((after - before) * fluid)
        before = jnp.where(lane < 16, turn(y_edge, -16 * a), turn(v, 16))
        after = jnp.where(lane >= 112, turn(y_edge, 16 * (4 - a)), turn(v, -16))
        grads.append((after - before) * fluid)
        before = jnp.where(deep == 0, turn(z_edge, -a), turn(v, 1))
        after = jnp.where(deep == 15, turn(z_edge, a), turn(v, -1))
        grads.append((after - before) * fluid)
    return grads


def exchange_kernel(
    n_gx,
    n_gy,
    counts_hbm,
    helper_hbm,
    vel_hbm,
    wall_hbm,
    base_hbm,
    extra_hbm,
    base_noise_hbm,
    extra_noise_hbm,
    base,
    extra,
    late_noise,
    tile_grad,
    own_total,
    moment_recv,
    counts,
    helper,
    vel,
    wall,
    base_noise,
    extra_noise,
    y_send,
    x_halo,
    y_halo,
    second,
    flow_own,
    flow_send,
    flow_recv,
    sum_own,
    extra_sum,
    sum_send,
    sum_recv,
    edge_own,
    edge_send,
    edge_recv,
    helper_grad,
    helper_relax,
    helper_total,
    row_total,
    relax,
    in_sem,
    tile_sem,
    halo_send_sem,
    halo_recv_sem,
    flow_send_sem,
    flow_recv_sem,
    sum_send_sem,
    sum_recv_sem,
    edge_send_sem,
    edge_recv_sem,
    moment_send_sem,
    moment_recv_sem,
):
    gx = lax.axis_index("gx")
    gy = lax.axis_index("gy")
    up_x, down_x = lax.rem(gx + 1, n_gx), lax.rem(gx + n_gx - 1, n_gx)
    up_y, down_y = lax.rem(gy + 1, n_gy), lax.rem(gy + n_gy - 1, n_gy)

    barrier = pltpu.get_barrier_semaphore()
    for k in range(1, n_gy):
        peer = lax.rem(gy + k, n_gy)
        pl.semaphore_signal(barrier, inc=1, device_id=(gx, peer), device_id_type=MESH)
    for peer in (up_x, down_x):
        pl.semaphore_signal(barrier, inc=1, device_id=(peer, gy), device_id_type=MESH)

    vel_copy = pltpu.make_async_copy(vel_hbm, vel, in_sem.at[0])
    wall_copy = pltpu.make_async_copy(wall_hbm, wall, in_sem.at[1])
    helper_copy = pltpu.make_async_copy(helper_hbm, helper, in_sem.at[7])
    counts_copy = pltpu.make_async_copy(counts_hbm, counts, in_sem.at[8])
    extra_copy = pltpu.make_async_copy(extra_hbm, extra, in_sem.at[2])
    base_copies = [
        pltpu.make_async_copy(base_hbm.at[t], base.at[t], tile_sem.at[t]) for t in range(TILES)
    ]
    base_noise_copies = [
        pltpu.make_async_copy(base_noise_hbm.at[:, 0], base_noise, in_sem.at[3]),
        pltpu.make_async_copy(base_noise_hbm.at[:, 1], late_noise, in_sem.at[4]),
    ]
    extra_noise_copies = [
        pltpu.make_async_copy(extra_noise_hbm.at[s], extra_noise.at[s], in_sem.at[5 + s])
        for s in range(STEPS)
    ]
    vel_copy.start()
    wall_copy.start()
    helper_copy.start()
    counts_copy.start()
    for copy in base_copies:
        copy.start()
    base_noise_copies[0].start()
    extra_copy.start()
    extra_noise_copies[0].start()
    extra_noise_copies[1].start()
    base_noise_copies[1].start()

    def send_all(src_of, dst_of, send_sem, recv_sem):
        copies = [
            pltpu.make_async_remote_copy(
                src_ref=src_of(k),
                dst_ref=dst_of(k),
                send_sem=send_sem(k),
                recv_sem=recv_sem(k),
                device_id=(gx, lax.rem(gy + k, n_gy)),
                device_id_type=MESH,
            )
            for k in range(1, n_gy)
        ]
        for copy in copies:
            copy.start()
        return copies

    def wanted(k):
        return lax.rem(helper[lax.rem(gy + k, n_gy)], TILES)

    sub = lax.broadcasted_iota(jnp.int32, (8, LANES), 0)
    lane = lax.broadcasted_iota(jnp.int32, (8, LANES), 1)
    block = lane // 16
    deep = lane % 16
    vel_copy.wait()
    for c in range(3):
        y_send[0, c] = vel[c, :, 7, :]
        y_send[1, c] = vel[c, :, 0, :]
    x_halo[6:] = jnp.zeros((2, 8, LANES), F32)
    flow = [swap_blocks([vel[a, :, y, :] for y in range(8)], block) for a in range(3)]
    for t in range(TILES):
        z_edge = jnp.zeros((8, LANES), F32)
        for a in range(3):
            if t > 0:
                z_edge = jnp.where(deep == a, pltpu.roll(flow[a][t - 1], 113 + a, 1), z_edge)
            if t < TILES - 1:
                z_edge = jnp.where(deep == 15 - a, pltpu.roll(flow[a][t + 1], 15 - a, 1), z_edge)
            flow_own[t, a] = flow[a][t]
        flow_own[t, 3] = z_edge
    wall_copy.wait()
    fluid = swap_blocks(
        [jnp.where(wall[:, y, :] == 0, 0.5 * time_step, 0.0).astype(F32) for y in range(8)], block
    )
    for t in range(TILES):
        flow_own[t, 4] = fluid[t]
    helper_copy.wait()
    counts_copy.wait()

    @pl.loop(0, n_gy)
    def _(k):
        flow_send[k] = flow_own[wanted(k)]

    pl.semaphore_wait(barrier, n_gy + 1)

    halo_copies = [
        pltpu.make_async_remote_copy(
            src_ref=src,
            dst_ref=dst,
            send_sem=halo_send_sem.at[i],
            recv_sem=halo_recv_sem.at[i],
            device_id=device,
            device_id_type=MESH,
        )
        for i, (src, dst, device) in enumerate(
            (
                (vel.at[:, 7], x_halo.at[0:3], (up_x, gy)),
                (vel.at[:, 0], x_halo.at[3:6], (down_x, gy)),
                (y_send.at[0], y_halo.at[0:3], (gx, up_y)),
                (y_send.at[1], y_halo.at[3:6], (gx, down_y)),
            )
        )
    ]
    for copy in halo_copies:
        copy.start()
    flow_copies = send_all(
        lambda k: flow_send.at[k],
        lambda k: flow_recv.at[k],
        lambda k: flow_send_sem.at[k],
        lambda k: flow_recv_sem.at[k],
    )
    flow_recv[0] = flow_send[0]

    my_slot = lax.rem(gy - helper[gy] // TILES + n_gy, n_gy)
    slots = [helper_slots(helper, gy, n_gy, t) for t in range(TILES)]

    for copy in base_copies:
        copy.wait()
    base_noise_copies[0].wait()

    @pl.loop(0, TILES)
    def _(t):
        for x in range(CHUNKS):
            lanes = pl.ds(x * LANES, LANES)
            state = [base[t, c, :, lanes] for c in range(3)]
            noise = [base_noise[t, c, :, lanes].astype(F32) for c in range(3)]
            for m, total in enumerate(products(state)):
                second[t, m, pl.ds(x, 1), :] = row_sum(total)
            for a in range(3):
                for b in range(3):
                    second[t, 6 + 3 * a + b, pl.ds(x, 1), :] = row_sum(fold(state[a] * noise[b]))
            second[t, 15, pl.ds(x, 1), :] = row_sum(inner(noise, noise))

    for t in range(TILES):
        sum_own[t] = second[t, 0] + second[t, 1] + second[t, 2]

    extra_copy.wait()

    @pl.loop(0, CHUNKS)
    def _(x):
        lanes = pl.ds(pl.multiple_of(x * LANES, LANES), LANES)
        total = jnp.zeros((8, LANES), F32)
        for f in range(EXTRA // GROUP):
            state = [extra[c, pl.ds(f * GROUP, GROUP), lanes] for c in range(3)]
            total = total + inner(state, state)
        extra_sum[pl.ds(x, 1), :] = row_sum(total)

    @pl.loop(0, n_gy)
    def _(k):
        sum_send[k, 0] = sum_own[wanted(k)]
        sum_send[k, 1] = extra_sum[...]

    sum_copies = send_all(
        lambda k: sum_send.at[k],
        lambda k: sum_recv.at[k],
        lambda k: sum_send_sem.at[k],
        lambda k: sum_recv_sem.at[k],
    )
    sum_recv[0] = sum_send[0]

    for copy in halo_copies:
        copy.wait_recv()
    low = jnp.where(gx > 0, 1.0, 0.0)
    high = jnp.where(gx < n_gx - 1, 1.0, 0.0)
    inside = jnp.where(sub < 3, low, high)
    x_edges = swap_blocks([x_halo[:, y, :] * inside for y in range(8)], block)
    sides = [jnp.where(gy > 0, y_halo[a], 0.0) for a in range(3)]
    sides += [jnp.where(gy < n_gy - 1, y_halo[3 + a], 0.0) for a in range(3)]
    sides += [jnp.zeros((8, LANES), F32)] * 2
    y_edges = swap_blocks(sides, block)
    for t in range(TILES):
        edge_own[t, 0] = y_edges[t]
        edge_own[t, 1] = x_edges[t]

    @pl.loop(0, TILES)
    def _(t):
        grads = gradient(
            [flow_own[t, a] for a in range(3)],
            flow_own[t, 3],
            flow_own[t, 4],
            edge_own[t, 0],
            edge_own[t, 1],
            sub,
            lane,
        )
        for c in range(9):
            tile_grad[t, c] = grads[c]
        mat = [[grads[3 * a + b] + (1.0 if a == b else 0.0) for b in range(3)] for a in range(3)]
        pairs = {}
        for m, (a, b) in enumerate(component_pairs):
            pairs[a, b] = pairs[b, a] = second[t, m]
        cross = [[second[t, 6 + 3 * a + b] for b in range(3)] for a in range(3)]
        once = noise_scale * (cross[0][0] + cross[1][1] + cross[2][2])
        twice = (noise_scale * noise_scale) * second[t, 15]
        for a in range(3):
            for b in range(3):
                inner_row = (
                    mat[a][0] * pairs[0, b] + mat[a][1] * pairs[1, b] + mat[a][2] * pairs[2, b]
                )
                once = once + (mat[a][b] * pairs[a, b])
                twice = twice + mat[a][b] * (inner_row + (2.0 * noise_scale) * cross[b][a])
        edge_own[t, 2] = once
        edge_own[t, 3] = twice

    @pl.loop(0, n_gy)
    def _(k):
        edge_send[k] = edge_own[wanted(k)]

    edge_copies = send_all(
        lambda k: edge_send.at[k],
        lambda k: edge_recv.at[k],
        lambda k: edge_send_sem.at[k],
        lambda k: edge_recv_sem.at[k],
    )
    edge_recv[0] = edge_send[0]

    for copy in sum_copies:
        copy.wait_recv()
    for t in range(TILES):
        slot, hit = slots[t]
        count = jnp.full((CHUNKS, LANES), counts[t], jnp.int32).astype(F32)
        total = sum_own[t] + jnp.where(hit == 1, sum_recv[slot, 1], 0.0)
        rate = relaxation(total, count)
        relax[t] = 1.0 - rate
        own_total[t] = edge_own[t, 3] - rate * (2.0 * edge_own[t, 2] - rate * sum_own[t])

    @pl.loop(0, TILES)
    def _(t):
        for x in range(CHUNKS):
            lanes = pl.ds(x * LANES, LANES)
            mat = matrix(lambda c: tile_grad[t, c, pl.ds(x, 1), :], relax[t, pl.ds(x, 1), :])
            state = [base[t, c, :, lanes] for c in range(3)]
            state = advance(mat, state, [base_noise[t, c, :, lanes] for c in range(3)])
            for c in range(3):
                base[t, c, :, lanes] = state[c]

    for copies in (flow_copies, edge_copies):
        for copy in copies:
            copy.wait_recv()
    grads = gradient(
        [flow_recv[my_slot, a] for a in range(3)],
        flow_recv[my_slot, 3],
        flow_recv[my_slot, 4],
        edge_recv[my_slot, 0],
        edge_recv[my_slot, 1],
        sub,
        lane,
    )
    for c in range(9):
        helper_grad[c] = grads[c]
    first = sum_recv[my_slot, 0]
    rate = relaxation(first + extra_sum[...], 256.0)
    helper_relax[...] = 1.0 - rate
    helper_total[...] = edge_recv[my_slot, 3] - rate * (2.0 * edge_recv[my_slot, 2] - rate * first)

    for copy in extra_noise_copies:
        copy.wait()
    moment_copies = []
    for p in range(PARTS):

        @pl.loop(0, ROWS)
        def _(r):
            x = p * ROWS + r
            lanes = pl.ds(pl.multiple_of(x * LANES, LANES), LANES)
            mat = matrix(
                lambda c: helper_grad[c, pl.ds(x, 1), :], helper_relax[pl.ds(x, 1), :]
            )
            total = jnp.zeros((8, LANES), F32)
            for f in range(EXTRA // GROUP):
                fields = pl.ds(f * GROUP, GROUP)
                state = [extra[c, fields, lanes] for c in range(3)]
                noise = [extra_noise[0, c, fields, lanes] for c in range(3)]
                state = advance(mat, state, noise)
                for c in range(3):
                    extra[c, fields, lanes] = state[c]
                total = total + inner(state, state)
            row_total[pl.ds(x, 1), :] = row_sum(total)

        rows = pl.ds(p * ROWS, ROWS)
        here = row_total[rows, :]
        moment_recv[0, p, 6] = here
        helper_relax[rows, :] = 1.0 - relaxation(here + helper_total[rows, :], 256.0)

        @pl.loop(0, ROWS)
        def _(r):
            x = p * ROWS + r
            lanes = pl.ds(pl.multiple_of(x * LANES, LANES), LANES)
            mat = matrix(
                lambda c: helper_grad[c, pl.ds(x, 1), :], helper_relax[pl.ds(x, 1), :]
            )
            totals = [jnp.zeros((8, LANES), F32) for _ in range(6)]
            for f in range(EXTRA // GROUP):
                fields = pl.ds(f * GROUP, GROUP)
                state = [extra[c, fields, lanes] for c in range(3)]
                noise = [extra_noise[1, c, fields, lanes] for c in range(3)]
                state = advance(mat, state, noise)
                for c in range(3):
                    extra[c, fields, lanes] = state[c]
                totals = [u + v for u, v in zip(totals, products(state))]
            for m in range(6):
                moment_recv[0, p, m, pl.ds(r, 1), :] = row_sum(totals[m])

        moment_copies.append(
            send_all(
                lambda k: moment_recv.at[0, p],
                lambda k: moment_recv.at[k, p],
                lambda k: moment_send_sem.at[p, k],
                lambda k: moment_recv_sem.at[p, k],
            )
        )

    base_noise_copies[1].wait()
    for copies in (halo_copies, flow_copies, sum_copies, edge_copies):
        for copy in copies:
            copy.wait_send()
    for copies in moment_copies:
        for copy in copies:
            copy.wait_recv()
            copy.wait_send()


def finish_kernel(
    n_gy,
    counts_hbm,
    helper_hbm,
    start,
    extra,
    noise,
    tile_grad,
    own_total,
    moment_recv,
    base_out,
    extra_out,
    stress_out,
    counts,
    helper,
    base,
    stress,
    staged,
    relax,
    moment,
    tile_sem,
    out_sem,
):
    gy = lax.axis_index("gy")
    helper_copy = pltpu.make_async_copy(helper_hbm, helper, out_sem.at[2])
    counts_copy = pltpu.make_async_copy(counts_hbm, counts, out_sem.at[3])
    extra_copy = pltpu.make_async_copy(extra, extra_out, out_sem.at[0])
    helper_copy.start()
    counts_copy.start()
    extra_copy.start()
    helper_copy.wait()
    counts_copy.wait()

    @pl.loop(0, TILES)
    def _(t):
        slot, hit = helper_slots(helper, gy, n_gy, t)
        heavy = hit == 1
        count = jnp.full((ROWS, LANES), counts[t], jnp.int32).astype(F32)
        for p in range(PARTS):
            total = own_total[t, pl.ds(p * ROWS, ROWS), :] + jnp.where(heavy, moment_recv[slot, p, 6], 0.0)
            relax[p] = relaxation(total, count)
        for x in range(CHUNKS):
            lanes = pl.ds(x * LANES, LANES)
            p, r = divmod(x, ROWS)
            mat = matrix(
                lambda c: tile_grad[t, c, pl.ds(x, 1), :], 1.0 - relax[p, pl.ds(r, 1), :]
            )
            state = [start[t, c, :, lanes] for c in range(3)]
            state = advance(mat, state, [noise[t, c, :, lanes] for c in range(3)])
            for c in range(3):
                base[t, c, :, lanes] = state[c]
            for m, total in enumerate(products(state)):
                moment[p, m, pl.ds(r, 1), :] = row_sum(total)
        pltpu.make_async_copy(base.at[t], base_out.at[t], tile_sem.at[t]).start()
        for p in range(PARTS):
            second = [
                (moment[p, m] + jnp.where(heavy, moment_recv[slot, p, m], 0.0)) / count
                for m in range(6)
            ]
            trace = second[0] + second[1] + second[2]
            stretch = 1.0 / (1.0 - trace / max_extension)
            for m in range(6):
                value = (stretch * second[m] - (1.0 if m < 3 else 0.0)) / weissenberg
                for r in range(ROWS):
                    staged[m, p * ROWS + r, pl.ds(t, 1), :] = value[r : r + 1]

    for m in range(6):
        for x in range(CHUNKS):
            stress[m, :, pl.ds(x * LANES, LANES)] = staged[m, x]
    stress_copy = pltpu.make_async_copy(stress, stress_out, out_sem.at[1])
    stress_copy.start()
    for t in range(TILES):
        pltpu.make_async_copy(base.at[t], base_out.at[t], tile_sem.at[t]).wait()
    extra_copy.wait()
    stress_copy.wait()


def hold(array):
    return pltpu.with_memory_space_constraint(array, pltpu.HBM)


def solution(mesh):
    n_gx, n_gy = mesh.shape["gx"], mesh.shape["gy"]

    def per_device(
        velocity,
        wall_cells,
        tile_counts,
        helper_tile,
        base_fields,
        extra_fields,
        base_noise,
        extra_noise,
    ):
        hbm = pl.BlockSpec(memory_space=pltpu.HBM)
        vmem = pl.BlockSpec(memory_space=pltpu.VMEM)
        dma = pltpu.SemaphoreType.DMA
        counts = hold(tile_counts.reshape(TILES))
        helper = hold(helper_tile.reshape(n_gy))

        def block(*lead):
            return pltpu.VMEM((*lead, CHUNKS, LANES), F32)

        passed = pl.pallas_call(
            functools.partial(exchange_kernel, n_gx, n_gy),
            out_shape=(
                jax.ShapeDtypeStruct((TILES, 3, BASE, CELLS), F32),
                jax.ShapeDtypeStruct((3, EXTRA, CELLS), F32),
                jax.ShapeDtypeStruct((TILES, 3, BASE, CELLS), jnp.bfloat16),
                jax.ShapeDtypeStruct((TILES, 9, CHUNKS, LANES), F32),
                jax.ShapeDtypeStruct((TILES, CHUNKS, LANES), F32),
                jax.ShapeDtypeStruct((n_gy, PARTS, 7, ROWS, LANES), F32),
            ),
            in_specs=[hbm] * 8,
            out_specs=(vmem,) * 6,
            scratch_shapes=[
                pltpu.SMEM((TILES,), jnp.int32),
                pltpu.SMEM((n_gy,), jnp.int32),
                block(3, 8),
                pltpu.VMEM((8, 8, LANES), jnp.int32),
                pltpu.VMEM((TILES, 3, BASE, CELLS), jnp.bfloat16),
                pltpu.VMEM((STEPS, 3, EXTRA, CELLS), jnp.bfloat16),
                block(2, 3),
                block(8),
                block(6),
                block(TILES, 16),
                block(TILES, 5),
                block(n_gy, 5),
                block(n_gy, 5),
                block(TILES),
                block(),
                block(n_gy, 2),
                block(n_gy, 2),
                block(TILES, 4),
                block(n_gy, 4),
                block(n_gy, 4),
                block(9),
                block(),
                block(),
                block(),
                block(TILES),
                dma((9,)),
                dma((TILES,)),
                dma((4,)),
                dma((4,)),
                dma((n_gy,)),
                dma((n_gy,)),
                dma((n_gy,)),
                dma((n_gy,)),
                dma((n_gy,)),
                dma((n_gy,)),
                dma((PARTS, n_gy)),
                dma((PARTS, n_gy)),
            ],
            compiler_params=pltpu.CompilerParams(
                collective_id=0, has_side_effects=True, vmem_limit_bytes=40 << 20
            ),
        )(
            counts,
            helper,
            hold(velocity),
            hold(wall_cells),
            hold(base_fields.reshape(TILES, 3, BASE, CELLS)),
            hold(extra_fields.reshape(3, EXTRA, CELLS)),
            hold(base_noise.reshape(TILES, STEPS, 3, BASE, CELLS)),
            hold(extra_noise.reshape(STEPS, 3, EXTRA, CELLS)),
        )
        base_out, extra_out, stress_out = pl.pallas_call(
            functools.partial(finish_kernel, n_gy),
            out_shape=(
                jax.ShapeDtypeStruct((TILES, 3, BASE, CELLS), F32),
                jax.ShapeDtypeStruct((3, EXTRA, CELLS), F32),
                jax.ShapeDtypeStruct((6, TILES, CELLS), F32),
            ),
            in_specs=[hbm] * 2 + [vmem] * 6,
            out_specs=(hbm,) * 3,
            scratch_shapes=[
                pltpu.SMEM((TILES,), jnp.int32),
                pltpu.SMEM((n_gy,), jnp.int32),
                pltpu.VMEM((TILES, 3, BASE, CELLS), F32),
                pltpu.VMEM((6, TILES, CELLS), F32),
                pltpu.VMEM((6, CHUNKS, TILES, LANES), F32),
                pltpu.VMEM((PARTS, ROWS, LANES), F32),
                pltpu.VMEM((PARTS, 6, ROWS, LANES), F32),
                dma((TILES,)),
                dma((4,)),
            ],
            compiler_params=pltpu.CompilerParams(vmem_limit_bytes=40 << 20),
        )(counts, helper, *passed)
        return base_out[None, None], extra_out[None, None], stress_out.transpose(1, 0, 2)[None, None]

    in_specs = (
        P(None, "gx", "gy", None),
        P("gx", "gy", None),
        P("gx", "gy", None),
        P("gx", None),
        P("gx", "gy", None, None, None, None),
        P("gx", "gy", None, None, None),
        P("gx", "gy", None, None, None, None, None),
        P("gx", "gy", None, None, None, None),
    )
    out_specs = (
        P("gx", "gy", None, None, None, None),
        P("gx", "gy", None, None, None),
        P("gx", "gy", None, None, None),
    )
    return jax.shard_map(
        per_device, mesh=mesh, in_specs=in_specs, out_specs=out_specs, check_vma=False
    )
```

time: 38.7 us -> 33 us (0.85)
  Pallas kernels: 38 us -> 32.3 us
    pallas_call x1, Pallas kernels: 34.2 us -> 28.5 us  [per_device(): pl.pallas_call(functools.partial(exchange_kernel, n_gx, n_gy), out_shape=...]
where the time goes in v3:
time: 33 us; the launch traced here: 32.9 us
  Pallas kernels  32.3 us (98%)
  between operations  0.64 us (2%)
    pallas_call x1, Pallas kernels, per_device(): pl.pallas_call(functools.partial(exchange_kernel, n_gx, n_gy), out_shape=...  28.5 us
    pallas_call x1, Pallas kernels, per_device(): pl.pallas_call(functools.partial(finish_kernel, n_gy), out_shape=(jax.Sha...  3.79 us

profile of v3, /device:TPU:32, one launch (start us, length us, event | category | flops | bytes accessed | tf_op | source)
XLA Modules:
  0.0 32.9 jit_solution(14675806843201938232)
XLA Ops:
  0.6 28.5 %shard_map.103 = (f32[8,3,32,1024]{3,2,1,0:T(8,128)S(1)}, f32[3,224,1024]{2,1,0:T(8,128)S(1)}, bf16[8,3,32,1024]{3,2,1,0:T(8,128)(2,1)S(1)}, f32[8,9,8,128]{3,2,...) custom-call(s32[8]{0:T(128)} %bitcast.15, s32[16]{0:T(128)} %bitcast.17, ...), custom_call_target="tpu_custom_call" | custom-call | tf_op jit(solution)/shard_map/pallas_call | solution.py:613
  29.1 3.8 %shard_map.104 = (f32[8,3,32,1024]{3,2,1,0:T(8,128)}, f32[3,224,1024]{2,1,0:T(8,128)}, f32[6,8,1024]{2,1,0:T(8,128)}) custom-call(s32[8]{0:T(128)} %bitcast.16, s32[16]{0:T(128)} %bitcast.18, f32[8,3,32,1024]{3,2,1,0:T(8,128)S(1)} %get-tuple-element.12.start, f32[3,224,1024]{2,1,0:T(8,128)S(1)} %get-tuple-element.13.extra, ...), custom_call_target="tpu_custom_call" | custom-call | tf_op jit(solution)/shard_map/pallas_call | solution.py:677

commit v4 on v3

--- a/solution.py
+++ b/solution.py
@@ -18,8 +18,7 @@
 BASE = 32
 EXTRA = 224
 GROUP = 32
-PARTS = 2
-ROWS = CHUNKS // PARTS
+HALF = 16
 
 time_step = 0.05
 weissenberg = 0.25
@@ -27,6 +26,9 @@
 noise_scale = (time_step / weissenberg) ** 0.5
 relax_scale = time_step * (0.5 / weissenberg)
 component_pairs = ((0, 0), (1, 1), (2, 2), (0, 1), (0, 2), (1, 2))
+early_pairs = [(i, j) for j in range(6) for i in range(j + 1)]
+late_pairs = [(i, j) for j in range(6, 9) for i in range(j + 1)]
+moment_at = {pair: n for n, pair in enumerate(early_pairs + late_pairs)}
 
 
 def wide(row):
@@ -135,16 +137,17 @@
     base_noise_hbm,
     extra_noise_hbm,
     base,
+    drifted,
     extra,
-    late_noise,
-    tile_grad,
     own_total,
+    own_rows,
     moment_recv,
     counts,
     helper,
     vel,
     wall,
     base_noise,
+    late_noise,
     extra_noise,
     y_send,
     x_halo,
@@ -160,10 +163,9 @@
     edge_own,
     edge_send,
     edge_recv,
-    helper_grad,
-    helper_relax,
-    helper_total,
-    row_total,
+    extra_second,
+    helper_map,
+    tile_grad,
     relax,
     in_sem,
     tile_sem,
@@ -402,6 +404,26 @@
     )
     edge_recv[0] = edge_send[0]
 
+    for copy in extra_noise_copies:
+        copy.wait()
+    for wanted_pairs in (early_pairs, late_pairs):
+
+        @pl.loop(0, CHUNKS)
+        def _(x):
+            lanes = pl.ds(pl.multiple_of(x * LANES, LANES), LANES)
+            totals = [jnp.zeros((8, LANES), F32) for _ in wanted_pairs]
+            for f in range(EXTRA // HALF):
+                fields = pl.ds(f * HALF, HALF)
+                parts = [extra[c, fields, lanes] for c in range(3)]
+                for s in range(STEPS):
+                    parts += [extra_noise[s, c, fields, lanes].astype(F32) for c in range(3)]
+                totals = [
+                    total + fold(parts[i] * parts[j])
+                    for total, (i, j) in zip(totals, wanted_pairs)
+                ]
+            for pair, total in zip(wanted_pairs, totals):
+                extra_second[moment_at[pair], pl.ds(x, 1), :] = row_sum(total)
+
     for copy in sum_copies:
         copy.wait_recv()
     for t in range(TILES):
@@ -434,77 +456,101 @@
         sub,
         lane,
     )
-    for c in range(9):
-        helper_grad[c] = grads[c]
     first = sum_recv[my_slot, 0]
     rate = relaxation(first + extra_sum[...], 256.0)
-    helper_relax[...] = 1.0 - rate
-    helper_total[...] = edge_recv[my_slot, 3] - rate * (2.0 * edge_recv[my_slot, 2] - rate * first)
-
-    for copy in extra_noise_copies:
-        copy.wait()
-    moment_copies = []
-    for p in range(PARTS):
-
-        @pl.loop(0, ROWS)
-        def _(r):
-            x = p * ROWS + r
-            lanes = pl.ds(pl.multiple_of(x * LANES, LANES), LANES)
-            mat = matrix(
-                lambda c: helper_grad[c, pl.ds(x, 1), :], helper_relax[pl.ds(x, 1), :]
-            )
-            total = jnp.zeros((8, LANES), F32)
-            for f in range(EXTRA // GROUP):
-                fields = pl.ds(f * GROUP, GROUP)
-                state = [extra[c, fields, lanes] for c in range(3)]
-                noise = [extra_noise[0, c, fields, lanes] for c in range(3)]
-                state = advance(mat, state, noise)
-                for c in range(3):
-                    extra[c, fields, lanes] = state[c]
-                total = total + inner(state, state)
-            row_total[pl.ds(x, 1), :] = row_sum(total)
-
-        rows = pl.ds(p * ROWS, ROWS)
-        here = row_total[rows, :]
-        moment_recv[0, p, 6] = here
-        helper_relax[rows, :] = 1.0 - relaxation(here + helper_total[rows, :], 256.0)
-
-        @pl.loop(0, ROWS)
-        def _(r):
-            x = p * ROWS + r
-            lanes = pl.ds(pl.multiple_of(x * LANES, LANES), LANES)
-            mat = matrix(
-                lambda c: helper_grad[c, pl.ds(x, 1), :], helper_relax[pl.ds(x, 1), :]
-            )
-            totals = [jnp.zeros((8, LANES), F32) for _ in range(6)]
-            for f in range(EXTRA // GROUP):
-                fields = pl.ds(f * GROUP, GROUP)
-                state = [extra[c, fields, lanes] for c in range(3)]
-                noise = [extra_noise[1, c, fields, lanes] for c in range(3)]
-                state = advance(mat, state, noise)
-                for c in range(3):
-                    extra[c, fields, lanes] = state[c]
-                totals = [u + v for u, v in zip(totals, products(state))]
-            for m in range(6):
-                moment_recv[0, p, m, pl.ds(r, 1), :] = row_sum(totals[m])
-
-        moment_copies.append(
-            send_all(
-                lambda k: moment_recv.at[0, p],
-                lambda k: moment_recv.at[k, p],
-                lambda k: moment_send_sem.at[p, k],
-                lambda k: moment_recv_sem.at[p, k],
-            )
-        )
+    own_share = edge_recv[my_slot, 3] - rate * (2.0 * edge_recv[my_slot, 2] - rate * first)
+
+    def pair_sum(i, j):
+        return extra_second[moment_at[min(i, j), max(i, j)]]
+
+    def step_matrix(keep):
+        return [
+            [grads[3 * a + b] + keep if a == b else grads[3 * a + b] for b in range(3)]
+            for a in range(3)
+        ]
+
+    def dot(left, right):
+        out = left[0] * right[0]
+        for u, v in zip(left[1:], right[1:]):
+            out = out + u * v
+        return out
+
+    one = step_matrix(1.0 - rate)
+    total = jnp.zeros((8, LANES), F32)
+    for a in range(3):
+        mixed = [
+            dot(one[a], [pair_sum(i, j) for i in range(3)]) + noise_scale * pair_sum(3 + a, j)
+            for j in (0, 1, 2, 3 + a)
+        ]
+        total = total + dot(one[a], mixed[:3]) + noise_scale * mixed[3]
+    moment_recv[0, 6] = total
+    two = step_matrix(1.0 - relaxation(total + own_share, 256.0))
+    combined = []
+    for a in range(3):
+        row = [dot(two[a], [one[c][b] for c in range(3)]) for b in range(3)]
+        row += [noise_scale * two[a][b] for b in range(3)]
+        combined.append(row)
+        for b in range(6):
+            helper_map[6 * a + b] = row[b]
+    for a in range(3):
+        mixed = [
+            dot(combined[a], [pair_sum(i, j) for i in range(6)]) + noise_scale * pair_sum(6 + a, j)
+            for j in range(9)
+        ]
+        for m, (first_axis, second_axis) in enumerate(component_pairs):
+            if first_axis == a:
+                moment_recv[0, m] = (
+                    dot(combined[second_axis], mixed[:6]) + noise_scale * mixed[6 + second_axis]
+                )
+
+    moment_copies = send_all(
+        lambda k: moment_recv.at[0],
+        lambda k: moment_recv.at[k],
+        lambda k: moment_send_sem.at[k],
+        lambda k: moment_recv_sem.at[k],
+    )
+
+    @pl.loop(0, CHUNKS)
+    def _(x):
+        lanes = pl.ds(pl.multiple_of(x * LANES, LANES), LANES)
+        rows = [
+            jnp.broadcast_to(helper_map[n, pl.ds(x, 1), :], (HALF, LANES)) for n in range(18)
+        ]
+        for f in range(EXTRA // HALF):
+            fields = pl.ds(f * HALF, HALF)
+            parts = [extra[c, fields, lanes] for c in range(3)]
+            parts += [extra_noise[0, c, fields, lanes].astype(F32) for c in range(3)]
+            for a in range(3):
+                last = extra_noise[1, a, fields, lanes].astype(F32)
+                extra[a, fields, lanes] = dot(rows[6 * a : 6 * a + 6], parts) + noise_scale * last
 
     base_noise_copies[1].wait()
+
+    @pl.loop(0, TILES)
+    def _(t):
+        for x in range(CHUNKS):
+            lanes = pl.ds(x * LANES, LANES)
+            mat = matrix(lambda c: tile_grad[t, c, pl.ds(x, 1), :], jnp.ones((1, LANES), F32))
+            state = [base[t, c, :, lanes] for c in range(3)]
+            moved = advance(mat, state, [late_noise[t, c, :, lanes] for c in range(3)])
+            for c in range(3):
+                drifted[t, c, :, lanes] = moved[c]
+            for m, (a, b) in enumerate(component_pairs):
+                here = pl.ds(x, 1)
+                own_rows[t, m, here, :] = row_sum(fold(moved[a] * moved[b]))
+                if a == b:
+                    own_rows[t, 6 + m, here, :] = 2.0 * row_sum(fold(moved[a] * state[a]))
+                else:
+                    both = fold(moved[a] * state[b] + moved[b] * state[a])
+                    own_rows[t, 6 + m, here, :] = row_sum(both)
+                own_rows[t, 12 + m, here, :] = row_sum(fold(state[a] * state[b]))
+
     for copies in (halo_copies, flow_copies, sum_copies, edge_copies):
         for copy in copies:
             copy.wait_send()
-    for copies in moment_copies:
-        for copy in copies:
-            copy.wait_recv()
-            copy.wait_send()
+    for copy in moment_copies:
+        copy.wait_recv()
+        copy.wait_send()
 
 
 def finish_kernel(
@@ -512,10 +558,10 @@
     counts_hbm,
     helper_hbm,
     start,
+    drifted,
     extra,
-    noise,
-    tile_grad,
     own_total,
+    own_rows,
     moment_recv,
     base_out,
     extra_out,
@@ -526,7 +572,6 @@
     stress,
     staged,
     relax,
-    moment,
     tile_sem,
     out_sem,
 ):
@@ -539,43 +584,38 @@
     extra_copy.start()
     helper_copy.wait()
     counts_copy.wait()
+    slots = [helper_slots(helper, gy, n_gy, t) for t in range(TILES)]
+    tile_counts = [jnp.full((CHUNKS, LANES), counts[t], jnp.int32).astype(F32) for t in range(TILES)]
+    for t in range(TILES):
+        slot, hit = slots[t]
+        total = own_total[t] + jnp.where(hit == 1, moment_recv[slot, 6], 0.0)
+        relax[t] = relaxation(total, tile_counts[t])
 
     @pl.loop(0, TILES)
     def _(t):
-        slot, hit = helper_slots(helper, gy, n_gy, t)
-        heavy = hit == 1
-        count = jnp.full((ROWS, LANES), counts[t], jnp.int32).astype(F32)
-        for p in range(PARTS):
-            total = own_total[t, pl.ds(p * ROWS, ROWS), :] + jnp.where(heavy, moment_recv[slot, p, 6], 0.0)
-            relax[p] = relaxation(total, count)
         for x in range(CHUNKS):
             lanes = pl.ds(x * LANES, LANES)
-            p, r = divmod(x, ROWS)
-            mat = matrix(
-                lambda c: tile_grad[t, c, pl.ds(x, 1), :], 1.0 - relax[p, pl.ds(r, 1), :]
-            )
-            state = [start[t, c, :, lanes] for c in range(3)]
-            state = advance(mat, state, [noise[t, c, :, lanes] for c in range(3)])
+            rate = wide(relax[t, pl.ds(x, 1), :])
             for c in range(3):
-                base[t, c, :, lanes] = state[c]
-            for m, total in enumerate(products(state)):
-                moment[p, m, pl.ds(r, 1), :] = row_sum(total)
+                base[t, c, :, lanes] = drifted[t, c, :, lanes] - rate * start[t, c, :, lanes]
         pltpu.make_async_copy(base.at[t], base_out.at[t], tile_sem.at[t]).start()
-        for p in range(PARTS):
-            second = [
-                (moment[p, m] + jnp.where(heavy, moment_recv[slot, p, m], 0.0)) / count
-                for m in range(6)
-            ]
-            trace = second[0] + second[1] + second[2]
-            stretch = 1.0 / (1.0 - trace / max_extension)
-            for m in range(6):
-                value = (stretch * second[m] - (1.0 if m < 3 else 0.0)) / weissenberg
-                for r in range(ROWS):
-                    staged[m, p * ROWS + r, pl.ds(t, 1), :] = value[r : r + 1]
+
+    for t in range(TILES):
+        slot, hit = slots[t]
+        rate = relax[t]
+        second = []
+        for m in range(6):
+            own = own_rows[t, m] - rate * (own_rows[t, 6 + m] - rate * own_rows[t, 12 + m])
+            second.append((own + jnp.where(hit == 1, moment_recv[slot, m], 0.0)) / tile_counts[t])
+        trace = second[0] + second[1] + second[2]
+        stretch = 1.0 / (1.0 - trace / max_extension)
+        for m in range(6):
+            staged[m, :, t, :] = (stretch * second[m] - (1.0 if m < 3 else 0.0)) / weissenberg
 
     for m in range(6):
         for x in range(CHUNKS):
             stress[m, :, pl.ds(x * LANES, LANES)] = staged[m, x]
+
     stress_copy = pltpu.make_async_copy(stress, stress_out, out_sem.at[1])
     stress_copy.start()
     for t in range(TILES):
@@ -614,11 +654,11 @@
             functools.partial(exchange_kernel, n_gx, n_gy),
             out_shape=(
                 jax.ShapeDtypeStruct((TILES, 3, BASE, CELLS), F32),
+                jax.ShapeDtypeStruct((TILES, 3, BASE, CELLS), F32),
                 jax.ShapeDtypeStruct((3, EXTRA, CELLS), F32),
-                jax.ShapeDtypeStruct((TILES, 3, BASE, CELLS), jnp.bfloat16),
-                jax.ShapeDtypeStruct((TILES, 9, CHUNKS, LANES), F32),
                 jax.ShapeDtypeStruct((TILES, CHUNKS, LANES), F32),
-                jax.ShapeDtypeStruct((n_gy, PARTS, 7, ROWS, LANES), F32),
+                jax.ShapeDtypeStruct((TILES, 18, CHUNKS, LANES), F32),
+                jax.ShapeDtypeStruct((n_gy, 7, CHUNKS, LANES), F32),
             ),
             in_specs=[hbm] * 8,
             out_specs=(vmem,) * 6,
@@ -627,6 +667,7 @@
                 pltpu.SMEM((n_gy,), jnp.int32),
                 block(3, 8),
                 pltpu.VMEM((8, 8, LANES), jnp.int32),
+                pltpu.VMEM((TILES, 3, BASE, CELLS), jnp.bfloat16),
                 pltpu.VMEM((TILES, 3, BASE, CELLS), jnp.bfloat16),
                 pltpu.VMEM((STEPS, 3, EXTRA, CELLS), jnp.bfloat16),
                 block(2, 3),
@@ -643,10 +684,9 @@
                 block(TILES, 4),
                 block(n_gy, 4),
                 block(n_gy, 4),
-                block(9),
-                block(),
-                block(),
-                block(),
+                block(45),
+                block(18),
+                block(TILES, 9),
                 block(TILES),
                 dma((9,)),
                 dma((TILES,)),
@@ -658,8 +698,8 @@
                 dma((n_gy,)),
                 dma((n_gy,)),
                 dma((n_gy,)),
-                dma((PARTS, n_gy)),
-                dma((PARTS, n_gy)),
+                dma((n_gy,)),
+                dma((n_gy,)),
             ],
             compiler_params=pltpu.CompilerParams(
                 collective_id=0, has_side_effects=True, vmem_limit_bytes=40 << 20
@@ -689,8 +729,7 @@
                 pltpu.VMEM((TILES, 3, BASE, CELLS), F32),
                 pltpu.VMEM((6, TILES, CELLS), F32),
                 pltpu.VMEM((6, CHUNKS, TILES, LANES), F32),
-                pltpu.VMEM((PARTS, ROWS, LANES), F32),
-                pltpu.VMEM((PARTS, 6, ROWS, LANES), F32),
+                block(TILES),
                 dma((TILES,)),
                 dma((4,)),
             ],

time: 33 us -> 30.1 us (0.912)
  Pallas kernels: 32.3 us -> 29.3 us
    pallas_call x1, Pallas kernels: 28.5 us -> 26.6 us  [per_device(): pl.pallas_call(functools.partial(exchange_kernel, n_gx, n_gy), out_shape=...]
    pallas_call x1, Pallas kernels: 3.79 us -> 2.73 us  [per_device(): pl.pallas_call(functools.partial(finish_kernel, n_gy), out_shape=(jax.Sha...]
where the time goes in v4:
time: 30.1 us; the launch traced here: 30 us
  Pallas kernels  29.3 us (97%)
  between operations  0.64 us (2%)
    pallas_call x1, Pallas kernels, per_device(): pl.pallas_call(functools.partial(exchange_kernel, n_gx, n_gy), out_shape=...  26.6 us
    pallas_call x1, Pallas kernels, per_device(): pl.pallas_call(functools.partial(finish_kernel, n_gy), out_shape=(jax.Sha...  2.73 us

profile of v4, /device:TPU:32, one launch (start us, length us, event | category | flops | bytes accessed | tf_op | source)
XLA Modules:
  0.0 30.0 jit_solution(17086688473096406218)
XLA Ops:
  0.6 26.6 %shard_map.103 = (f32[8,3,32,1024]{3,2,1,0:T(8,128)S(1)}, f32[8,3,32,1024]{3,2,1,0:T(8,128)S(1)}, f32[3,224,1024]{2,1,0:T(8,128)S(1)}, f32[8,8,128]{2,1,0:T(8,12...) custom-call(s32[8]{0:T(128)} %bitcast.15, s32[16]{0:T(128)} %bitcast.17, f32[3,8,8,128]{3,2,1,0:T(8,128)} %vel_hbm.1, ...), custom_call_target="tpu_custom_call" | custom-call | tf_op jit(solution)/shard_map/pallas_call | solution.py:653
  27.2 2.7 %shard_map.104 = (f32[8,3,32,1024]{3,2,1,0:T(8,128)}, f32[3,224,1024]{2,1,0:T(8,128)}, f32[6,8,1024]{2,1,0:T(8,128)}) custom-call(s32[8]{0:T(128)} %bitcast.16, s32[16]{0:T(128)} %bitcast.18, f32[8,3,32,1024]{3,2,1,0:T(8,128)S(1)} %get-tuple-element.12.start, f32[8,3,32,1024]{3,2,1,0:T(8,128)S(1)} %get-tuple-element.13.drifted, ...), custom_call_target="tpu_custom_call" | custom-call | tf_op jit(solution)/shard_map/pallas_call | solution.py:717

commit v5 on v4

--- a/solution.py
+++ b/solution.py
@@ -78,11 +78,31 @@
     return relax_scale * (1.0 / (1.0 - total / count / max_extension))
 
 
+SIDE = 4
+offsets = sorted(
+    range(1, SIDE * SIDE), key=lambda k: -sum(min(v, SIDE - v) for v in divmod(k, SIDE))
+)
+
+
+def wrap(value):
+    return lax.rem(value + SIDE, SIDE)
+
+
+def shifted(gy, k):
+    x, y = gy // SIDE, lax.rem(gy, SIDE)
+    return wrap(x + k // SIDE) * SIDE + wrap(y + k % SIDE)
+
+
+def slot_from(gy, sender):
+    x, y = gy // SIDE, lax.rem(gy, SIDE)
+    return wrap(x - sender // SIDE) * SIDE + wrap(y - lax.rem(sender, SIDE))
+
+
 def helper_slots(helper, gy, n_gy, t):
     slot, hit = jnp.int32(0), jnp.int32(0)
     for h in range(n_gy):
         match = helper[h] == gy * TILES + t
-        slot = jnp.where(match, lax.rem(gy - h + n_gy, n_gy), slot)
+        slot = jnp.where(match, slot_from(gy, h), slot)
         hit = jnp.where(match, 1, hit)
     return slot, hit
 
@@ -153,6 +173,7 @@
     x_halo,
     y_halo,
     second,
+    layer_own,
     flow_own,
     flow_send,
     flow_recv,
@@ -179,6 +200,7 @@
     edge_recv_sem,
     moment_send_sem,
     moment_recv_sem,
+    ring_sem,
 ):
     gx = lax.axis_index("gx")
     gy = lax.axis_index("gy")
@@ -186,11 +208,11 @@
     up_y, down_y = lax.rem(gy + 1, n_gy), lax.rem(gy + n_gy - 1, n_gy)
 
     barrier = pltpu.get_barrier_semaphore()
-    for k in range(1, n_gy):
-        peer = lax.rem(gy + k, n_gy)
-        pl.semaphore_signal(barrier, inc=1, device_id=(gx, peer), device_id_type=MESH)
-    for peer in (up_x, down_x):
-        pl.semaphore_signal(barrier, inc=1, device_id=(peer, gy), device_id_type=MESH)
+    near = [(gx, up_y), (gx, down_y), (up_x, gy), (down_x, gy)]
+    near += [(gx, shifted(gy, v)) for v in range(1, SIDE)]
+    near += [(gx, shifted(gy, v * SIDE)) for v in range(1, SIDE)]
+    for device in near:
+        pl.semaphore_signal(barrier, inc=1, device_id=device, device_id_type=MESH)
 
     vel_copy = pltpu.make_async_copy(vel_hbm, vel, in_sem.at[0])
     wall_copy = pltpu.make_async_copy(wall_hbm, wall, in_sem.at[1])
@@ -227,17 +249,17 @@
                 dst_ref=dst_of(k),
                 send_sem=send_sem(k),
                 recv_sem=recv_sem(k),
-                device_id=(gx, lax.rem(gy + k, n_gy)),
+                device_id=(gx, shifted(gy, k)),
                 device_id_type=MESH,
             )
-            for k in range(1, n_gy)
+            for k in offsets
         ]
         for copy in copies:
             copy.start()
         return copies
 
     def wanted(k):
-        return lax.rem(helper[lax.rem(gy + k, n_gy)], TILES)
+        return lax.rem(helper[shifted(gy, k)], TILES)
 
     sub = lax.broadcasted_iota(jnp.int32, (8, LANES), 0)
     lane = lax.broadcasted_iota(jnp.int32, (8, LANES), 1)
@@ -264,14 +286,21 @@
     )
     for t in range(TILES):
         flow_own[t, 4] = fluid[t]
+    sides = [y_send[0, a] for a in range(3)] + [y_send[1, a] for a in range(3)]
+    layers = swap_blocks(sides + [jnp.zeros((8, LANES), F32)] * 2, block)
+    for t in range(TILES):
+        layer_own[t] = layers[t]
     helper_copy.wait()
     counts_copy.wait()
 
     @pl.loop(0, n_gy)
     def _(k):
-        flow_send[k] = flow_own[wanted(k)]
-
-    pl.semaphore_wait(barrier, n_gy + 1)
+        tile = wanted(k)
+        flow_send[k] = flow_own[tile]
+        mine = helper[shifted(gy, k)] // TILES == gy
+        flow_send[k, 0] = jnp.where(mine, flow_own[tile, 0], layer_own[tile])
+
+    pl.semaphore_wait(barrier, len(near))
 
     halo_copies = [
         pltpu.make_async_remote_copy(
@@ -293,6 +322,11 @@
     ]
     for copy in halo_copies:
         copy.start()
+    for v in range(1, SIDE):
+        pl.semaphore_signal(
+            ring_sem, inc=1, device_id=(gx, shifted(gy, v)), device_id_type=MESH
+        )
+    pl.semaphore_wait(ring_sem, SIDE - 1)
     flow_copies = send_all(
         lambda k: flow_send.at[k],
         lambda k: flow_recv.at[k],
@@ -301,7 +335,10 @@
     )
     flow_recv[0] = flow_send[0]
 
-    my_slot = lax.rem(gy - helper[gy] // TILES + n_gy, n_gy)
+    owner = helper[gy] // TILES
+    my_slot = slot_from(gy, owner)
+    low_slot = slot_from(gy, lax.rem(owner + n_gy - 1, n_gy))
+    high_slot = slot_from(gy, lax.rem(owner + 1, n_gy))
     slots = [helper_slots(helper, gy, n_gy, t) for t in range(TILES)]
 
     for copy in base_copies:
@@ -359,8 +396,8 @@
     sides += [jnp.zeros((8, LANES), F32)] * 2
     y_edges = swap_blocks(sides, block)
     for t in range(TILES):
-        edge_own[t, 0] = y_edges[t]
-        edge_own[t, 1] = x_edges[t]
+        layer_own[t] = y_edges[t]
+        edge_own[t, 0] = x_edges[t]
 
     @pl.loop(0, TILES)
     def _(t):
@@ -368,8 +405,8 @@
             [flow_own[t, a] for a in range(3)],
             flow_own[t, 3],
             flow_own[t, 4],
+            layer_own[t],
             edge_own[t, 0],
-            edge_own[t, 1],
             sub,
             lane,
         )
@@ -389,8 +426,8 @@
                 )
                 once = once + (mat[a][b] * pairs[a, b])
                 twice = twice + mat[a][b] * (inner_row + (2.0 * noise_scale) * cross[b][a])
-        edge_own[t, 2] = once
-        edge_own[t, 3] = twice
+        edge_own[t, 1] = once
+        edge_own[t, 2] = twice
 
     @pl.loop(0, n_gy)
     def _(k):
@@ -424,41 +461,25 @@
             for pair, total in zip(wanted_pairs, totals):
                 extra_second[moment_at[pair], pl.ds(x, 1), :] = row_sum(total)
 
-    for copy in sum_copies:
-        copy.wait_recv()
-    for t in range(TILES):
-        slot, hit = slots[t]
-        count = jnp.full((CHUNKS, LANES), counts[t], jnp.int32).astype(F32)
-        total = sum_own[t] + jnp.where(hit == 1, sum_recv[slot, 1], 0.0)
-        rate = relaxation(total, count)
-        relax[t] = 1.0 - rate
-        own_total[t] = edge_own[t, 3] - rate * (2.0 * edge_own[t, 2] - rate * sum_own[t])
-
-    @pl.loop(0, TILES)
-    def _(t):
-        for x in range(CHUNKS):
-            lanes = pl.ds(x * LANES, LANES)
-            mat = matrix(lambda c: tile_grad[t, c, pl.ds(x, 1), :], relax[t, pl.ds(x, 1), :])
-            state = [base[t, c, :, lanes] for c in range(3)]
-            state = advance(mat, state, [base_noise[t, c, :, lanes] for c in range(3)])
-            for c in range(3):
-                base[t, c, :, lanes] = state[c]
-
-    for copies in (flow_copies, edge_copies):
+    for copies in (sum_copies, flow_copies, edge_copies):
         for copy in copies:
             copy.wait_recv()
     grads = gradient(
         [flow_recv[my_slot, a] for a in range(3)],
         flow_recv[my_slot, 3],
         flow_recv[my_slot, 4],
+        jnp.where(
+            block < 3,
+            jnp.where(owner > 0, flow_recv[low_slot, 0], 0.0),
+            jnp.where(owner < n_gy - 1, flow_recv[high_slot, 0], 0.0),
+        ),
         edge_recv[my_slot, 0],
-        edge_recv[my_slot, 1],
         sub,
         lane,
     )
     first = sum_recv[my_slot, 0]
     rate = relaxation(first + extra_sum[...], 256.0)
-    own_share = edge_recv[my_slot, 3] - rate * (2.0 * edge_recv[my_slot, 2] - rate * first)
+    own_share = edge_recv[my_slot, 2] - rate * (2.0 * edge_recv[my_slot, 1] - rate * first)
 
     def pair_sum(i, j):
         return extra_second[moment_at[min(i, j), max(i, j)]]
@@ -524,6 +545,14 @@
                 last = extra_noise[1, a, fields, lanes].astype(F32)
                 extra[a, fields, lanes] = dot(rows[6 * a : 6 * a + 6], parts) + noise_scale * last
 
+    for t in range(TILES):
+        slot, hit = slots[t]
+        count = jnp.full((CHUNKS, LANES), counts[t], jnp.int32).astype(F32)
+        total = sum_own[t] + jnp.where(hit == 1, sum_recv[slot, 1], 0.0)
+        rate = relaxation(total, count)
+        relax[t] = rate
+        own_total[t] = edge_own[t, 2] - rate * (2.0 * edge_own[t, 1] - rate * sum_own[t])
+
     base_noise_copies[1].wait()
 
     @pl.loop(0, TILES)
@@ -531,7 +560,12 @@
         for x in range(CHUNKS):
             lanes = pl.ds(x * LANES, LANES)
             mat = matrix(lambda c: tile_grad[t, c, pl.ds(x, 1), :], jnp.ones((1, LANES), F32))
-            state = [base[t, c, :, lanes] for c in range(3)]
+            rate = wide(relax[t, pl.ds(x, 1), :])
+            start = [base[t, c, :, lanes] for c in range(3)]
+            state = advance(mat, start, [base_noise[t, c, :, lanes] for c in range(3)])
+            state = [state[c] - rate * start[c] for c in range(3)]
+            for c in range(3):
+                base[t, c, :, lanes] = state[c]
             moved = advance(mat, state, [late_noise[t, c, :, lanes] for c in range(3)])
             for c in range(3):
                 drifted[t, c, :, lanes] = moved[c]
@@ -674,6 +708,7 @@
                 block(8),
                 block(6),
                 block(TILES, 16),
+                block(TILES),
                 block(TILES, 5),
                 block(n_gy, 5),
                 block(n_gy, 5),
@@ -681,9 +716,9 @@
                 block(),
                 block(n_gy, 2),
                 block(n_gy, 2),
-                block(TILES, 4),
-                block(n_gy, 4),
-                block(n_gy, 4),
+                block(TILES, 3),
+                block(n_gy, 3),
+                block(n_gy, 3),
                 block(45),
                 block(18),
                 block(TILES, 9),
@@ -700,6 +735,7 @@
                 dma((n_gy,)),
                 dma((n_gy,)),
                 dma((n_gy,)),
+                pltpu.SemaphoreType.REGULAR,
             ],
             compiler_params=pltpu.CompilerParams(
                 collective_id=0, has_side_effects=True, vmem_limit_bytes=40 << 20

time: 30.1 us -> 28.6 us (0.950)
  Pallas kernels: 29.3 us -> 27.8 us
    pallas_call x1, Pallas kernels: 26.6 us -> 25 us  [per_device(): pl.pallas_call(functools.partial(exchange_kernel, n_gx, n_gy), out_shape=...]
where the time goes in v5:
time: 28.6 us; the launch traced here: 28.4 us
  Pallas kernels  27.8 us (97%)
  between operations  0.64 us (2%)
    pallas_call x1, Pallas kernels, per_device(): pl.pallas_call(functools.partial(exchange_kernel, n_gx, n_gy), out_shape=...  25 us
    pallas_call x1, Pallas kernels, per_device(): pl.pallas_call(functools.partial(finish_kernel, n_gy), out_shape=(jax.Sha...  2.73 us

profile of v5, /device:TPU:32, one launch (start us, length us, event | category | flops | bytes accessed | tf_op | source)
XLA Modules:
  0.0 28.4 jit_solution(6330180963586076545)
XLA Ops:
  0.6 25.0 %shard_map.103 = (f32[8,3,32,1024]{3,2,1,0:T(8,128)S(1)}, f32[8,3,32,1024]{3,2,1,0:T(8,128)S(1)}, f32[3,224,1024]{2,1,0:T(8,128)S(1)}, f32[8,8,128]{2,1,0:T(8,12...) custom-call(s32[8]{0:T(128)} %bitcast.15, s32[16]{0:T(128)} %bitcast.17, f32[3,8,8,128]{3,2,1,0:T(8,128)} %vel_hbm.1, ...), custom_call_target="tpu_custom_call" | custom-call | tf_op jit(solution)/shard_map/pallas_call | solution.py:687
  25.7 2.7 %shard_map.104 = (f32[8,3,32,1024]{3,2,1,0:T(8,128)}, f32[3,224,1024]{2,1,0:T(8,128)}, f32[6,8,1024]{2,1,0:T(8,128)}) custom-call(s32[8]{0:T(128)} %bitcast.16, s32[16]{0:T(128)} %bitcast.18, f32[8,3,32,1024]{3,2,1,0:T(8,128)S(1)} %get-tuple-element.12.start, f32[8,3,32,1024]{3,2,1,0:T(8,128)S(1)} %get-tuple-element.13.drifted, ...), custom_call_target="tpu_custom_call" | custom-call | tf_op jit(solution)/shard_map/pallas_call | solution.py:753

commit v6 on v5

--- a/solution.py
+++ b/solution.py
@@ -179,7 +179,6 @@
     flow_recv,
     sum_own,
     extra_sum,
-    sum_send,
     sum_recv,
     edge_own,
     edge_send,
@@ -258,9 +257,6 @@
             copy.start()
         return copies
 
-    def wanted(k):
-        return lax.rem(helper[shifted(gy, k)], TILES)
-
     sub = lax.broadcasted_iota(jnp.int32, (8, LANES), 0)
     lane = lax.broadcasted_iota(jnp.int32, (8, LANES), 1)
     block = lane // 16
@@ -269,6 +265,32 @@
     for c in range(3):
         y_send[0, c] = vel[c, :, 7, :]
         y_send[1, c] = vel[c, :, 0, :]
+    pl.semaphore_wait(barrier, len(near))
+
+    halo_copies = [
+        pltpu.make_async_remote_copy(
+            src_ref=src,
+            dst_ref=dst,
+            send_sem=halo_send_sem.at[i],
+            recv_sem=halo_recv_sem.at[i],
+            device_id=device,
+            device_id_type=MESH,
+        )
+        for i, (src, dst, device) in enumerate(
+            (
+                (y_send.at[0], y_halo.at[0:3], (gx, up_y)),
+                (y_send.at[1], y_halo.at[3:6], (gx, down_y)),
+                (vel.at[:, 7], x_halo.at[0:3], (up_x, gy)),
+                (vel.at[:, 0], x_halo.at[3:6], (down_x, gy)),
+            )
+        )
+    ]
+    for copy in halo_copies:
+        copy.start()
+    for v in range(1, SIDE):
+        pl.semaphore_signal(
+            ring_sem, inc=1, device_id=(gx, shifted(gy, v)), device_id_type=MESH
+        )
     x_halo[6:] = jnp.zeros((2, 8, LANES), F32)
     flow = [swap_blocks([vel[a, :, y, :] for y in range(8)], block) for a in range(3)]
     for t in range(TILES):
@@ -293,39 +315,13 @@
     helper_copy.wait()
     counts_copy.wait()
 
-    @pl.loop(0, n_gy)
-    def _(k):
-        tile = wanted(k)
-        flow_send[k] = flow_own[tile]
-        mine = helper[shifted(gy, k)] // TILES == gy
-        flow_send[k, 0] = jnp.where(mine, flow_own[tile, 0], layer_own[tile])
-
-    pl.semaphore_wait(barrier, len(near))
-
-    halo_copies = [
-        pltpu.make_async_remote_copy(
-            src_ref=src,
-            dst_ref=dst,
-            send_sem=halo_send_sem.at[i],
-            recv_sem=halo_recv_sem.at[i],
-            device_id=device,
-            device_id_type=MESH,
-        )
-        for i, (src, dst, device) in enumerate(
-            (
-                (vel.at[:, 7], x_halo.at[0:3], (up_x, gy)),
-                (vel.at[:, 0], x_halo.at[3:6], (down_x, gy)),
-                (y_send.at[0], y_halo.at[0:3], (gx, up_y)),
-                (y_send.at[1], y_halo.at[3:6], (gx, down_y)),
-            )
-        )
-    ]
-    for copy in halo_copies:
-        copy.start()
-    for v in range(1, SIDE):
-        pl.semaphore_signal(
-            ring_sem, inc=1, device_id=(gx, shifted(gy, v)), device_id_type=MESH
-        )
+    named = [helper[shifted(gy, k)] for k in range(n_gy)]
+    wanted = [lax.rem(name, TILES) for name in named]
+    for k in range(n_gy):
+        mine = named[k] // TILES == gy
+        flow_send[k, 0] = jnp.where(mine, flow_own[wanted[k], 0], layer_own[wanted[k]])
+        flow_send[k, 1:] = flow_own[wanted[k], 1:]
+
     pl.semaphore_wait(ring_sem, SIDE - 1)
     flow_copies = send_all(
         lambda k: flow_send.at[k],
@@ -361,30 +357,6 @@
     for t in range(TILES):
         sum_own[t] = second[t, 0] + second[t, 1] + second[t, 2]
 
-    extra_copy.wait()
-
-    @pl.loop(0, CHUNKS)
-    def _(x):
-        lanes = pl.ds(pl.multiple_of(x * LANES, LANES), LANES)
-        total = jnp.zeros((8, LANES), F32)
-        for f in range(EXTRA // GROUP):
-            state = [extra[c, pl.ds(f * GROUP, GROUP), lanes] for c in range(3)]
-            total = total + inner(state, state)
-        extra_sum[pl.ds(x, 1), :] = row_sum(total)
-
-    @pl.loop(0, n_gy)
-    def _(k):
-        sum_send[k, 0] = sum_own[wanted(k)]
-        sum_send[k, 1] = extra_sum[...]
-
-    sum_copies = send_all(
-        lambda k: sum_send.at[k],
-        lambda k: sum_recv.at[k],
-        lambda k: sum_send_sem.at[k],
-        lambda k: sum_recv_sem.at[k],
-    )
-    sum_recv[0] = sum_send[0]
-
     for copy in halo_copies:
         copy.wait_recv()
     low = jnp.where(gx > 0, 1.0, 0.0)
@@ -399,8 +371,7 @@
         layer_own[t] = y_edges[t]
         edge_own[t, 0] = x_edges[t]
 
-    @pl.loop(0, TILES)
-    def _(t):
+    for t in range(TILES):
         grads = gradient(
             [flow_own[t, a] for a in range(3)],
             flow_own[t, 3],
@@ -428,10 +399,10 @@
                 twice = twice + mat[a][b] * (inner_row + (2.0 * noise_scale) * cross[b][a])
         edge_own[t, 1] = once
         edge_own[t, 2] = twice
-
-    @pl.loop(0, n_gy)
-    def _(k):
-        edge_send[k] = edge_own[wanted(k)]
+        edge_own[t, 3] = sum_own[t]
+
+    for k in range(n_gy):
+        edge_send[k] = edge_own[wanted[k]]
 
     edge_copies = send_all(
         lambda k: edge_send.at[k],
@@ -441,6 +412,7 @@
     )
     edge_recv[0] = edge_send[0]
 
+    extra_copy.wait()
     for copy in extra_noise_copies:
         copy.wait()
     for wanted_pairs in (early_pairs, late_pairs):
@@ -461,7 +433,21 @@
             for pair, total in zip(wanted_pairs, totals):
                 extra_second[moment_at[pair], pl.ds(x, 1), :] = row_sum(total)
 
-    for copies in (sum_copies, flow_copies, edge_copies):
+        if wanted_pairs is early_pairs:
+            extra_sum[...] = (
+                extra_second[moment_at[0, 0]]
+                + extra_second[moment_at[1, 1]]
+                + extra_second[moment_at[2, 2]]
+            )
+            sum_copies = send_all(
+                lambda k: extra_sum,
+                lambda k: sum_recv.at[k],
+                lambda k: sum_send_sem.at[k],
+                lambda k: sum_recv_sem.at[k],
+            )
+            sum_recv[0] = extra_sum[...]
+
+    for copies in (flow_copies, edge_copies):
         for copy in copies:
             copy.wait_recv()
     grads = gradient(
@@ -477,7 +463,7 @@
         sub,
         lane,
     )
-    first = sum_recv[my_slot, 0]
+    first = edge_recv[my_slot, 3]
     rate = relaxation(first + extra_sum[...], 256.0)
     own_share = edge_recv[my_slot, 2] - rate * (2.0 * edge_recv[my_slot, 1] - rate * first)
 
@@ -545,10 +531,12 @@
                 last = extra_noise[1, a, fields, lanes].astype(F32)
                 extra[a, fields, lanes] = dot(rows[6 * a : 6 * a + 6], parts) + noise_scale * last
 
+    for copy in sum_copies:
+        copy.wait_recv()
     for t in range(TILES):
         slot, hit = slots[t]
         count = jnp.full((CHUNKS, LANES), counts[t], jnp.int32).astype(F32)
-        total = sum_own[t] + jnp.where(hit == 1, sum_recv[slot, 1], 0.0)
+        total = sum_own[t] + jnp.where(hit == 1, sum_recv[slot], 0.0)
         rate = relaxation(total, count)
         relax[t] = rate
         own_total[t] = edge_own[t, 2] - rate * (2.0 * edge_own[t, 1] - rate * sum_own[t])
@@ -714,11 +702,10 @@
                 block(n_gy, 5),
                 block(TILES),
                 block(),
-                block(n_gy, 2),
-                block(n_gy, 2),
-                block(TILES, 3),
-                block(n_gy, 3),
-                block(n_gy, 3),
+                block(n_gy),
+                block(TILES, 4),
+                block(n_gy, 4),
+                block(n_gy, 4),
                 block(45),
                 block(18),
                 block(TILES, 9),

time: 28.6 us -> 27.8 us (0.972)
  Pallas kernels: 27.8 us -> 27 us
    pallas_call x1, Pallas kernels: 25 us -> 24.3 us  [per_device(): pl.pallas_call(functools.partial(exchange_kernel, n_gx, n_gy), out_shape=...]
where the time goes in v6:
time: 27.8 us; the launch traced here: 27.6 us
  Pallas kernels  27 us (97%)
  between operations  0.64 us (2%)
    pallas_call x1, Pallas kernels, per_device(): pl.pallas_call(functools.partial(exchange_kernel, n_gx, n_gy), out_shape=...  24.3 us
    pallas_call x1, Pallas kernels, per_device(): pl.pallas_call(functools.partial(finish_kernel, n_gy), out_shape=(jax.Sha...  2.73 us

profile of v6, /device:TPU:32, one launch (start us, length us, event | category | flops | bytes accessed | tf_op | source)
XLA Modules:
  0.0 27.6 jit_solution(1261250145598287014)
XLA Ops:
  0.6 24.3 %shard_map.103 = (f32[8,3,32,1024]{3,2,1,0:T(8,128)S(1)}, f32[8,3,32,1024]{3,2,1,0:T(8,128)S(1)}, f32[3,224,1024]{2,1,0:T(8,128)S(1)}, f32[8,8,128]{2,1,0:T(8,12...) custom-call(s32[8]{0:T(128)} %bitcast.15, s32[16]{0:T(128)} %bitcast.17, f32[3,8,8,128]{3,2,1,0:T(8,128)} %vel_hbm.1, ...), custom_call_target="tpu_custom_call" | custom-call | tf_op jit(solution)/shard_map/pallas_call | solution.py:675
  24.9 2.7 %shard_map.104 = (f32[8,3,32,1024]{3,2,1,0:T(8,128)}, f32[3,224,1024]{2,1,0:T(8,128)}, f32[6,8,1024]{2,1,0:T(8,128)}) custom-call(s32[8]{0:T(128)} %bitcast.16, s32[16]{0:T(128)} %bitcast.18, f32[8,3,32,1024]{3,2,1,0:T(8,128)S(1)} %get-tuple-element.12.start, f32[8,3,32,1024]{3,2,1,0:T(8,128)S(1)} %get-tuple-element.13.drifted, ...), custom_call_target="tpu_custom_call" | custom-call | tf_op jit(solution)/shard_map/pallas_call | solution.py:740

commit v7 on v6

--- a/solution.py
+++ b/solution.py
@@ -98,13 +98,16 @@
     return wrap(x - sender // SIDE) * SIDE + wrap(y - lax.rem(sender, SIDE))
 
 
-def helper_slots(helper, gy, n_gy, t):
-    slot, hit = jnp.int32(0), jnp.int32(0)
-    for h in range(n_gy):
-        match = helper[h] == gy * TILES + t
-        slot = jnp.where(match, slot_from(gy, h), slot)
-        hit = jnp.where(match, 1, hit)
-    return slot, hit
+def helper_slots(helper, gy, n_gy):
+    place = [helper[h] - gy * TILES for h in range(n_gy)]
+    sender = [slot_from(gy, h) for h in range(n_gy)]
+    slots = []
+    for t in range(TILES):
+        slot = jnp.int32(-1)
+        for h in range(n_gy):
+            slot = jnp.where(place[h] == t, sender[h], slot)
+        slots.append((jnp.maximum(slot, 0), slot >= 0))
+    return slots
 
 
 def swap_blocks(regs, block):
@@ -335,7 +338,7 @@
     my_slot = slot_from(gy, owner)
     low_slot = slot_from(gy, lax.rem(owner + n_gy - 1, n_gy))
     high_slot = slot_from(gy, lax.rem(owner + 1, n_gy))
-    slots = [helper_slots(helper, gy, n_gy, t) for t in range(TILES)]
+    slots = helper_slots(helper, gy, n_gy)
 
     for copy in base_copies:
         copy.wait()
@@ -497,8 +500,6 @@
         row = [dot(two[a], [one[c][b] for c in range(3)]) for b in range(3)]
         row += [noise_scale * two[a][b] for b in range(3)]
         combined.append(row)
-        for b in range(6):
-            helper_map[6 * a + b] = row[b]
     for a in range(3):
         mixed = [
             dot(combined[a], [pair_sum(i, j) for i in range(6)]) + noise_scale * pair_sum(6 + a, j)
@@ -516,6 +517,10 @@
         lambda k: moment_send_sem.at[k],
         lambda k: moment_recv_sem.at[k],
     )
+
+    for a in range(3):
+        for b in range(6):
+            helper_map[6 * a + b] = combined[a][b]
 
     @pl.loop(0, CHUNKS)
     def _(x):
@@ -536,7 +541,7 @@
     for t in range(TILES):
         slot, hit = slots[t]
         count = jnp.full((CHUNKS, LANES), counts[t], jnp.int32).astype(F32)
-        total = sum_own[t] + jnp.where(hit == 1, sum_recv[slot], 0.0)
+        total = sum_own[t] + jnp.where(hit, sum_recv[slot], 0.0)
         rate = relaxation(total, count)
         relax[t] = rate
         own_total[t] = edge_own[t, 2] - rate * (2.0 * edge_own[t, 1] - rate * sum_own[t])
@@ -606,11 +611,11 @@
     extra_copy.start()
     helper_copy.wait()
     counts_copy.wait()
-    slots = [helper_slots(helper, gy, n_gy, t) for t in range(TILES)]
+    slots = helper_slots(helper, gy, n_gy)
     tile_counts = [jnp.full((CHUNKS, LANES), counts[t], jnp.int32).astype(F32) for t in range(TILES)]
     for t in range(TILES):
         slot, hit = slots[t]
-        total = own_total[t] + jnp.where(hit == 1, moment_recv[slot, 6], 0.0)
+        total = own_total[t] + jnp.where(hit, moment_recv[slot, 6], 0.0)
         relax[t] = relaxation(total, tile_counts[t])
 
     @pl.loop(0, TILES)
@@ -628,7 +633,7 @@
         second = []
         for m in range(6):
             own = own_rows[t, m] - rate * (own_rows[t, 6 + m] - rate * own_rows[t, 12 + m])
-            second.append((own + jnp.where(hit == 1, moment_recv[slot, m], 0.0)) / tile_counts[t])
+            second.append((own + jnp.where(hit, moment_recv[slot, m], 0.0)) / tile_counts[t])
         trace = second[0] + second[1] + second[2]
         stretch = 1.0 / (1.0 - trace / max_extension)
         for m in range(6):

time: 27.8 us -> 27.7 us (level)
  no operation moved by 1% of the time
where the time goes in v7:
time: 27.7 us; the launch traced here: 27.6 us
  Pallas kernels  27 us (97%)
  between operations  0.64 us (2%)
    pallas_call x1, Pallas kernels, per_device(): pl.pallas_call(functools.partial(exchange_kernel, n_gx, n_gy), out_shape=...  24.3 us
    pallas_call x1, Pallas kernels, per_device(): pl.pallas_call(functools.partial(finish_kernel, n_gy), out_shape=(jax.Sha...  2.7 us

profile of v7, /device:TPU:32, one launch (start us, length us, event | category | flops | bytes accessed | tf_op | source)
XLA Modules:
  0.0 27.6 jit_solution(6354848428506955075)
XLA Ops:
  0.6 24.3 %shard_map.103 = (f32[8,3,32,1024]{3,2,1,0:T(8,128)S(1)}, f32[8,3,32,1024]{3,2,1,0:T(8,128)S(1)}, f32[3,224,1024]{2,1,0:T(8,128)S(1)}, f32[8,8,128]{2,1,0:T(8,12...) custom-call(s32[8]{0:T(128)} %bitcast.15, s32[16]{0:T(128)} %bitcast.17, f32[3,8,8,128]{3,2,1,0:T(8,128)} %vel_hbm.1, ...), custom_call_target="tpu_custom_call" | custom-call | tf_op jit(solution)/shard_map/pallas_call | solution.py:680
  24.9 2.7 %shard_map.104 = (f32[8,3,32,1024]{3,2,1,0:T(8,128)}, f32[3,224,1024]{2,1,0:T(8,128)}, f32[6,8,1024]{2,1,0:T(8,128)}) custom-call(s32[8]{0:T(128)} %bitcast.16, s32[16]{0:T(128)} %bitcast.18, f32[8,3,32,1024]{3,2,1,0:T(8,128)S(1)} %get-tuple-element.12.start, f32[8,3,32,1024]{3,2,1,0:T(8,128)S(1)} %get-tuple-element.13.drifted, ...), custom_call_target="tpu_custom_call" | custom-call | tf_op jit(solution)/shard_map/pallas_call | solution.py:745
